TPU v7x, 128 devices: a whole 4x4x4 slice. The times are simulated.
128 devices in a mesh: dp: 4 (over y_hi, core), tx: 4 (over x), ty: 8 (over y_lo, z).
Axes of the slice: x: 4, y: 4 (y_hi: 2, y_lo: 2; y = y_hi * 2 + y_lo), z: 4, core: 2. Of those that a mesh axis runs over, the one named last changes fastest.
Arguments:
- frames: bfloat16 [4, 12288, 1024], P('dp', ('tx', 'ty')), may hold values from -6 to 6
- first_conv_weight: bfloat16 [1024, 4096], replicated, may hold values from -0.125 to 0.125
- first_residual_projection: bfloat16 [1024, 1024], replicated, may hold values from -0.1875 to 0.1875
- second_conv_weight: bfloat16 [1024, 4096], replicated, may hold values from -0.125 to 0.125
- second_residual_projection: bfloat16 [1024, 1024], replicated, may hold values from -0.1875 to 0.1875
- out_grad: bfloat16 [4, 12288, 1024], P('dp', ('tx', 'ty')), may hold values from -6 to 6
Outputs:
- output_frames: bfloat16 [4, 12288, 1024], P('dp', ('tx', 'ty'))
- frame_grad: bfloat16 [4, 12288, 1024], P('dp', ('tx', 'ty'))
- conv_first_grad: float32 [1024, 4096], P('ty')
- proj_first_grad: float32 [1024, 1024], P('ty')
- conv_second_grad: float32 [1024, 4096], P('ty')
- proj_second_grad: float32 [1024, 1024], P('ty')
All inputs are finite; a program needn't handle non-finite values.
Results may differ from a plain program's by a relative error of at most 0.023.
Values may be sent and summed in bfloat16 or wider, within the bound.
A program may use at most 128 MiB of HBM per device.

v0:
```python
import jax
import jax.numpy as jnp
from jax import lax
from jax.sharding import PartitionSpec as P

NEAR_DILATION = 64


def shifted_2(value, axis, steps):
    count = lax.axis_size(axis)
    leading, last = (max(0, -steps), min(count, count - steps))
    return lax.ppermute(value, axis, [(source, source + steps) for source in range(leading, last)])


def mult_trans(left, right):
    return lax.dot_general(
        left, right, (((1,), (1,)), ((), ())), preferred_element_type=jnp.float32
    )


def contract_rows(left, right):
    return lax.dot_general(
        left, right, (((0,), (0,)), ((), ())), preferred_element_type=jnp.float32
    )


def fetch_near(input_frames):
    frame_rows = input_frames.shape[0]
    boundary_frames = shifted_2(input_frames[frame_rows - NEAR_DILATION :], ("tx", "ty"), 1)
    return jnp.concatenate([boundary_frames, input_frames[: frame_rows - NEAR_DILATION]], 0)


def fetch_far(input_frames):
    result = shifted_2(input_frames, ("tx", "ty"), lax.axis_size("ty"))
    return result


def back_near(value_rows):
    boundary_frames = shifted_2(value_rows[:NEAR_DILATION], ("tx", "ty"), -1)
    return jnp.concatenate([value_rows[NEAR_DILATION:], boundary_frames], 0)


def back_far(value_rows):
    result = shifted_2(value_rows, ("tx", "ty"), -lax.axis_size("ty"))
    return result


def causal_parts(input_frames, shifted, conv_weight, proj_weight):
    width = input_frames.shape[1]
    pre = jnp.dot(shifted, conv_weight[:, : 2 * width], preferred_element_type=jnp.float32)
    pre = pre + jnp.dot(
        input_frames, conv_weight[:, 2 * width :], preferred_element_type=jnp.float32
    )
    tanh_part = jnp.tanh(pre[:, :width])
    gate_part = jax.nn.sigmoid(pre[:, width:])
    gated = (tanh_part * gate_part).astype(jnp.bfloat16)
    output = (
        input_frames.astype(jnp.float32)
        + jnp.dot(gated, proj_weight, preferred_element_type=jnp.float32)
    ).astype(jnp.bfloat16)
    return (output, tanh_part, gate_part, gated)


def backward_layer_pass(tanh_part, gate_part, grad_out, conv_weight, proj_weight, send_back):
    width = grad_out.shape[1]
    grad_gated = mult_trans(grad_out, proj_weight)
    grad_pre = jnp.concatenate(
        [
            grad_gated * gate_part * (1.0 - tanh_part * tanh_part),
            grad_gated * tanh_part * gate_part * (1.0 - gate_part),
        ],
        1,
    ).astype(jnp.bfloat16)
    tap_weight = conv_weight[:, : 2 * width]
    tap_part = send_back(mult_trans(grad_pre, tap_weight).astype(jnp.bfloat16))
    grad_in = grad_out.astype(jnp.float32) + mult_trans(grad_pre, conv_weight[:, 2 * width :])
    grad_in = (grad_in + tap_part.astype(jnp.float32)).astype(jnp.bfloat16)
    return (grad_in, grad_pre)


def weight_grads(shifted, input_frames, grad_pre, gated, grad_out):
    frame_rows = input_frames.shape[0]
    width = input_frames.shape[1]
    streams = lax.axis_size("dp")
    scale = float(streams * lax.axis_size(("tx", "ty")) * frame_rows) ** (-0.5)
    share = lax.psum_scatter(
        jnp.concatenate(
            [
                contract_rows(shifted, grad_pre),
                contract_rows(input_frames, grad_pre),
                contract_rows(gated, grad_out),
            ],
            1,
        ).astype(jnp.bfloat16),
        "ty",
        scatter_dimension=0,
        tiled=True,
    )
    total = lax.psum(share, ("dp", "tx")).astype(jnp.float32)
    total = total * scale
    return (total[:, : 4 * width], total[:, 4 * width :])


def shards(
    frames,
    first_conv_weight,
    first_residual_projection,
    second_conv_weight,
    second_residual_projection,
    out_grad,
):
    block_input = frames[0]
    output_gradient = out_grad[0]
    near_input = fetch_near(block_input)
    middle_activation, first_tanh_filter, first_gate, first_gated_value = causal_parts(
        block_input, near_input, first_conv_weight, first_residual_projection
    )
    far_input = fetch_far(middle_activation)
    block_output, second_tanh_filter, second_gate, second_gated_value = causal_parts(
        middle_activation, far_input, second_conv_weight, second_residual_projection
    )
    middle_gradient, second_preactivation = backward_layer_pass(
        second_tanh_filter,
        second_gate,
        output_gradient,
        second_conv_weight,
        second_residual_projection,
        back_far,
    )
    conv_two_grad, proj_two_grad = weight_grads(
        far_input, middle_activation, second_preactivation, second_gated_value, output_gradient
    )
    input_gradient, first_preactivation = backward_layer_pass(
        first_tanh_filter,
        first_gate,
        middle_gradient,
        first_conv_weight,
        first_residual_projection,
        back_near,
    )
    conv_one_grad, proj_one_grad = weight_grads(
        near_input, block_input, first_preactivation, first_gated_value, middle_gradient
    )
    return (
        block_output[None],
        input_gradient[None],
        conv_one_grad,
        proj_one_grad,
        conv_two_grad,
        proj_two_grad,
    )


def solution(mesh):
    return jax.shard_map(
        shards,
        mesh=mesh,
        in_specs=(P("dp", ("tx", "ty"), None), P(), P(), P(), P(), P("dp", ("tx", "ty"), None)),
        out_specs=(
            P("dp", ("tx", "ty"), None),
            P("dp", ("tx", "ty"), None),
            P("ty", None),
            P("ty", None),
            P("ty", None),
            P("ty", None),
        ),
        check_vma=False,
    )
```

profile of v0, /device:TPU:1, one launch (start us, length us, event | category | flops | bytes accessed | tf_op | source)
XLA Modules:
  0.0 449.8 jit_solution(8395511374280914642)
XLA Ops:
  8.3 4.6 %collective-permute-start = (bf16[64,1024]{1,0:T(8,128)(2,1)S(1)}, bf16[64,1024]{1,0:T(8,128)(2,1)S(1)}, u32[]{:S(2)}, u32[]{:S(2)}) collective-permute-start(bf16[64,1024]{1,0:T(8,128)(2,1)S(1)} %slice_bitcast_fusion.1), channel_id=1, source_target_pairs={{0,1},{1,2},{2,3},{3,4},{4,5},{5,6},{6,7},{7,8},{8,9},{9,10},{10,1... | collective-permute-start | bytes 393224 | tf_op jit(solution)/shard_map/ppermute | solution.py:12
  12.9 4.2 fusion.10
  17.3 1.8 fusion.16
  19.8 2.7 copy-done.7
  23.5 4.8 %collective-permute-start.1 = (bf16[384,1024]{1,0:T(8,128)(2,1)S(1)}, bf16[384,1024]{1,0:T(8,128)(2,1)S(1)}, u32[]{:S(2)}, u32[]{:S(2)}) collective-permute-start(bf16[384,1024]{1,0:T(8,128)(2,1)S(1)} %add_convert_fusion.3), channel_id=1, source_target_pairs={{0,8},{1,9},{2,10},{3,11},{4,12},{5,13},{6,14},{7,15},{8,16},{9,17... | collective-permute-start | bytes 2359304 | tf_op jit(solution)/shard_map/ppermute | solution.py:12
  28.3 1.8 fusion.2
  30.2 13.6 %collective-permute-done.1 = bf16[384,1024]{1,0:T(8,128)(2,1)S(1)} collective-permute-done((bf16[384,1024]{1,0:T(8,128)(2,1)S(1)}, bf16[384,1024]{1,0:T(8,128)(2,1)S(1)}, u32[]{:S(2)}, u32[]{:S(2)}) %collective-permute-start.1) | collective-permute-done | bytes 786464 | tf_op jit(solution)/shard_map/ppermute | solution.py:12
  43.7 1.8 fusion.19
  45.5 1.7 multiply_convert_fusion.3
  48.6 2.4 convolution_convert_fusion
  51.0 2.4 convolution_convert_fusion.1
  53.4 5.7 %pad_maximum_fusion.1 = bf16[1024,5120]{1,0:T(8,128)(2,1)} fusion(bf16[1024,1024]{1,0:T(8,128)(2,1)S(1)} %convolution_convert_fusion.3, bf16[1024,2048]{1,0:T(8,128)(2,1)S(1)} %convolution_convert_fusion, bf16[1024,2048]{1,0:T(8,128)(2,1)S(1)} %convolution_convert_fusion.1), kind=kLoop, calls=%fused_computation.1 | loop fusion | flops 31457280 | bytes 20971520 | tf_op jit(solution)/shard_map/concatenate | solution.py:87
  59.1 4.6 %fusion.33 = bf16[384,1024]{1,0:T(8,128)(2,1)S(1)} fusion(bf16[1024,4096]{1,0:T(8,128)(2,1)} %param.9, bf16[384,1024]{1,0:T(8,128)(2,1)} %copy-done.21, bf16[384,1024]{1,0:T(8,128)(2,1)} %copy-done.19), kind=kOutput, calls=%fused_computation.51 | convolution fusion | flops 1614151680 | bytes 6553600 | tf_op jit(solution)/shard_map/dot_general | solution.py:16
  63.8 1.8 collective-permute-start.2
  65.6 18.6 %collective-permute-done.2 = bf16[384,1024]{1,0:T(8,128)(2,1)S(1)} collective-permute-done((bf16[384,1024]{1,0:T(8,128)(2,1)S(1)}, bf16[384,1024]{1,0:T(8,128)(2,1)S(1)}, u32[]{:S(2)}, u32[]{:S(2)}) %collective-permute-start.2) | collective-permute-done | bytes 786464 | tf_op jit(solution)/shard_map/ppermute | solution.py:12
  84.2 4.1 add_convert_fusion.1
  88.3 1.5 multiply_convert_fusion.1
  89.9 2.4 convolution_convert_fusion.2
  92.3 1.3 convolution_convert_fusion.4
  93.7 2.4 convert_bitcast_fusion
  96.1 5.6 %pad_maximum_fusion = bf16[1024,5120]{1,0:T(8,128)(2,1)} fusion(bf16[1024,1024]{1,0:T(8,128)(2,1)S(1)} %convolution_convert_fusion.4, bf16[1024,2048]{1,0:T(8,128)(2,1)S(1)} %convert_bitcast_fusion, bf16[1024,2048]{1,0:T(8,128)(2,1)S(1)} %convolution_convert_fusion.2), kind=kLoop, calls=%fused_computation | loop fusion | flops 31457280 | bytes 20971520 | tf_op jit(solution)/shard_map/concatenate | solution.py:87
  101.8 72.9 %reduce-scatter.5.cloned.1.call-done = bf16[128,5120]{1,0:T(8,128)(2,1)} async-done(((bf16[1024,5120]{1,0:T(8,128)(2,1)}), bf16[128,5120]{1,0:T(8,128)(2,1)}) %reduce-scatter.5.cloned.1.call-update) | async-done | bytes 1310736 | tf_op jit(solution)/shard_map/reduce_scatter | solution.py:86
  174.7 113.8 %reduce-scatter.3.cloned.1.call-done = bf16[128,5120]{1,0:T(8,128)(2,1)} async-done(((bf16[1024,5120]{1,0:T(8,128)(2,1)}), bf16[128,5120]{1,0:T(8,128)(2,1)}) %reduce-scatter.3.cloned.1.call-update) | async-done | bytes 1310736 | tf_op jit(solution)/shard_map/reduce_scatter | solution.py:86
  288.6 4.4 fusion.30
  293.0 1.7 collective-permute-start.3
  294.7 1.9 fusion.36
  296.6 2.7 collective-permute-done.3
  299.4 5.0 %fusion.37 = bf16[1,384,1024]{2,1,0:T(8,128)(2,1)} fusion(bf16[384,1024]{1,0:T(8,128)(2,1)S(1)} %copy-done.18, bf16[64,1024]{1,0:T(8,128)(2,1)S(1)} %collective-permute-done.3, bf16[320,1024]{1,0:T(8,128)(2,1)S(1)} %slice.80, bf16[1024,4096]{1,0:T(8,128)(2,1)} %param.7, bf16[384,1024]{1,0:T(8,128)(2,1)S(1)} %copy-done.26, bf16[384,1024]{1,0:T(8,128)(2,1)S(1)} %copy-done.24), kind=kOutput, calls=%fused_computation.53 | convolution fusion | flops 1616904192 | bytes 8126464 | tf_op jit(solution)/shard_map/dot_general | solution.py:16
  304.3 132.0 %all-reduce.3.cloned.1.call-done = (bf16[128,5120]{1,0:T(8,128)(2,1)}, bf16[128,5120]{1,0:T(8,128)(2,1)}) async-done(((bf16[128,5120]{1,0:T(8,128)(2,1)}, bf16[128,5120]{1,0:T(8,128)(2,1)}), (bf16[128,5120]{1,0:T(8,128)(2,1)}, bf16[128,5120]{1,0:T(8,128)(2,1)})) %all-reduce.3.cloned.1.call-update) | async-done | bytes 2621456 | tf_op jit(solution)/shard_map/psum | solution.py:99
  436.3 2.3 convert_multiply_fusion
  438.6 1.5 slice.82
  441.0 1.5 slice.84
  (74 shorter events, 6.1 us)
Async XLA Ops:
  7.2 38.4 %copy-start = (bf16[1024,1024]{1,0:T(8,128)(2,1)S(1)}, bf16[1024,1024]{1,0:T(8,128)(2,1)}, u32[]{:S(2)}) copy-start(bf16[1024,1024]{1,0:T(8,128)(2,1)} %param.10) | copy-start | bytes 6291460
  7.2 167.5 %reduce-scatter.5.cloned.1.call-start = ((), (), s32[]{:S(2)}) async-start(), calls=%async_computation.3 | async-start | bytes 11796480 | tf_op jit(solution)/shard_map/reduce_scatter | solution.py:86
  8.3 8.9 %copy-start.3 = (bf16[1,384,1024]{2,1,0:T(8,128)(2,1)S(1)}, bf16[1,384,1024]{2,1,0:T(8,128)(2,1)}, u32[]{:S(2)}) copy-start(bf16[1,384,1024]{2,1,0:T(8,128)(2,1)} %param.6) | copy-start | bytes 2359300
  8.3 9.0 %copy-start.6 = (bf16[1024,4096]{1,0:T(8,128)(2,1)S(1)}, bf16[1024,4096]{1,0:T(8,128)(2,1)}, u32[]{:S(2)}) copy-start(bf16[1024,4096]{1,0:T(8,128)(2,1)} %param.7) | copy-start | bytes 25165828
  8.3 9.0 %collective-permute-start = (bf16[64,1024]{1,0:T(8,128)(2,1)S(1)}, bf16[64,1024]{1,0:T(8,128)(2,1)S(1)}, u32[]{:S(2)}, u32[]{:S(2)}) collective-permute-start(bf16[64,1024]{1,0:T(8,128)(2,1)S(1)} %slice_bitcast_fusion.1), channel_id=1, source_target_pairs={{0,1},{1,2},{2,3},{3,4},{4,5},{5,6},{6,7},{7,8},{8,9},{9,10},{10,1... | collective-permute-start | bytes 393224 | tf_op jit(solution)/shard_map/ppermute | solution.py:12
  17.2 11.1 %slice-start = ((s8[8388608]{0:T(1024)(128)(4,1)}), s8[4194304]{0:T(1024)(128)(4,1)S(1)}, s32[]{:S(2)}) async-start(s8[8388608]{0:T(1024)(128)(4,1)} %bitcast.38), calls=%async_computation.5 | async-start | bytes 8388608
  17.3 11.1 %slice-start.1 = ((s8[8388608]{0:T(1024)(128)(4,1)}), s8[4194304]{0:T(1024)(128)(4,1)S(1)}, s32[]{:S(2)}) async-start(s8[8388608]{0:T(1024)(128)(4,1)} %bitcast.38), calls=%async_computation.6 | async-start | bytes 8388608
  19.1 4.3 copy-start.1
  19.1 3.3 copy-start.7
  23.5 25.1 %copy-start.11 = (bf16[384,1024]{1,0:T(8,128)(2,1)}, bf16[384,1024]{1,0:T(8,128)(2,1)S(1)}, u32[]{:S(2)}) copy-start(bf16[384,1024]{1,0:T(8,128)(2,1)S(1)} %add_convert_fusion.3) | copy-start | bytes 2359300
  23.5 20.3 %collective-permute-start.1 = (bf16[384,1024]{1,0:T(8,128)(2,1)S(1)}, bf16[384,1024]{1,0:T(8,128)(2,1)S(1)}, u32[]{:S(2)}, u32[]{:S(2)}) collective-permute-start(bf16[384,1024]{1,0:T(8,128)(2,1)S(1)} %add_convert_fusion.3), channel_id=1, source_target_pairs={{0,8},{1,9},{2,10},{3,11},{4,12},{5,13},{6,14},{7,15},{8,16},{9,17... | collective-permute-start | bytes 2359304 | tf_op jit(solution)/shard_map/ppermute | solution.py:12
  30.1 15.4 %copy-start.9 = (bf16[1,384,1024]{2,1,0:T(8,128)(2,1)S(1)}, bf16[1,384,1024]{2,1,0:T(8,128)(2,1)}, u32[]{:S(2)}) copy-start(bf16[1,384,1024]{2,1,0:T(8,128)(2,1)} %param.11) | copy-start | bytes 2359300
  47.2 3.7 copy-start.19
  47.2 3.7 copy-start.21
  59.0 229.5 %reduce-scatter.3.cloned.1.call-start = ((), (), s32[]{:S(2)}) async-start(), calls=%async_computation.2 | async-start | bytes 11796480 | tf_op jit(solution)/shard_map/reduce_scatter | solution.py:86
  59.1 25.1 %copy-start.10 = (bf16[1,384,1024]{2,1,0:T(8,128)(2,1)S(1)}, bf16[1,384,1024]{2,1,0:T(8,128)(2,1)}, u32[]{:S(2)}) copy-start(bf16[1,384,1024]{2,1,0:T(8,128)(2,1)} %param.11) | copy-start | bytes 2359300
  59.1 25.1 %copy-start.20 = (bf16[384,1024]{1,0:T(8,128)(2,1)S(1)}, bf16[384,1024]{1,0:T(8,128)(2,1)}, u32[]{:S(2)}) copy-start(bf16[384,1024]{1,0:T(8,128)(2,1)} %copy-done.19) | copy-start | bytes 2359300
  59.1 25.1 %copy-start.22 = (bf16[384,1024]{1,0:T(8,128)(2,1)S(1)}, bf16[384,1024]{1,0:T(8,128)(2,1)}, u32[]{:S(2)}) copy-start(bf16[384,1024]{1,0:T(8,128)(2,1)} %copy-done.21) | copy-start | bytes 2359300
  63.8 24.5 %copy-start.2 = (f32[384,2048]{1,0:T(8,128)S(1)}, f32[384,2048]{1,0:T(8,128)}, u32[]{:S(2)}) copy-start(f32[384,2048]{1,0:T(8,128)} %copy-done.1) | copy-start | bytes 9437188
  63.8 24.5 %copy-start.8 = (bf16[1024,1024]{1,0:T(8,128)(2,1)S(1)}, bf16[1024,1024]{1,0:T(8,128)(2,1)}, u32[]{:S(2)}) copy-start(bf16[1024,1024]{1,0:T(8,128)(2,1)} %param.8) | copy-start | bytes 6291460
  63.8 20.4 %collective-permute-start.2 = (bf16[384,1024]{1,0:T(8,128)(2,1)S(1)}, bf16[384,1024]{1,0:T(8,128)(2,1)S(1)}, u32[]{:S(2)}, u32[]{:S(2)}) collective-permute-start(bf16[384,1024]{1,0:T(8,128)(2,1)S(1)} %fusion.33), channel_id=1, source_target_pairs={{8,0},{9,1},{10,2},{11,3},{12,4},{13,5},{14,6},{15,7},{16,8},{17,9... | collective-permute-start | bytes 2359304 | tf_op jit(solution)/shard_map/ppermute | solution.py:12
  88.3 4.0 copy-start.17
  89.8 3.8 copy-start.23
  89.9 3.8 copy-start.25
  89.9 2.4 copy-start.5
  101.7 186.8 %copy-start.24 = (bf16[384,1024]{1,0:T(8,128)(2,1)S(1)}, bf16[384,1024]{1,0:T(8,128)(2,1)}, u32[]{:S(2)}) copy-start(bf16[384,1024]{1,0:T(8,128)(2,1)} %copy-done.23) | copy-start | bytes 2359300
  101.7 334.6 %all-reduce.3.cloned.1.call-start = ((), (), s32[]{:S(2)}) async-start(), calls=%async_computation.4 | async-start | bytes 5242880 | tf_op jit(solution)/shard_map/psum | solution.py:99
  288.6 6.1 %copy-start.12 = (bf16[384,1024]{1,0:T(8,128)(2,1)S(1)}, bf16[384,1024]{1,0:T(8,128)(2,1)}, u32[]{:S(2)}) copy-start(bf16[384,1024]{1,0:T(8,128)(2,1)} %copy-done.11) | copy-start | bytes 2359300
  288.6 6.1 %copy-start.16 = (bf16[384,1024]{1,0:T(8,128)(2,1)S(1)}, bf16[384,1024]{1,0:T(8,128)(2,1)}, u32[]{:S(2)}) copy-start(bf16[384,1024]{1,0:T(8,128)(2,1)} %copy-done.15) | copy-start | bytes 2359300
  293.0 6.4 %copy-start.18 = (bf16[384,1024]{1,0:T(8,128)(2,1)S(1)}, bf16[384,1024]{1,0:T(8,128)(2,1)}, u32[]{:S(2)}) copy-start(bf16[384,1024]{1,0:T(8,128)(2,1)} %copy-done.17) | copy-start | bytes 2359300
  293.0 6.4 %copy-start.26 = (bf16[384,1024]{1,0:T(8,128)(2,1)S(1)}, bf16[384,1024]{1,0:T(8,128)(2,1)}, u32[]{:S(2)}) copy-start(bf16[384,1024]{1,0:T(8,128)(2,1)} %copy-done.25) | copy-start | bytes 2359300
  293.0 6.3 %collective-permute-start.3 = (bf16[64,1024]{1,0:T(8,128)(2,1)S(1)}, bf16[64,1024]{1,0:T(8,128)(2,1)S(1)}, u32[]{:S(2)}, u32[]{:S(2)}) collective-permute-start(bf16[64,1024]{1,0:T(8,128)(2,1)S(1)} %slice.81), channel_id=1, source_target_pairs={{1,0},{2,1},{3,2},{4,3},{5,4},{6,5},{7,6},{8,7},{9,8},{10,9},{11,1... | collective-permute-start | bytes 393224 | tf_op jit(solution)/shard_map/ppermute | solution.py:12
  (4 other events, 5.7 us)
Sparse Core Ops, SparseCore 0:
  59.2 115.4 reduce-scatter.4
  177.1 111.3 reduce-scatter.2
  291.1 145.1 all-reduce.2
where the time goes:
time: 452 us; the launch traced here: 450 us
  waiting for transfers between devices  354 us (78%)
  matrix products  45.9 us (10%)
  between operations  14.4 us (3%)
  other arithmetic  14.2 us (3%)
  starting transfers between devices  13.1 us (3%)
  local copies, waits for them, and re-layouts  8.62 us (2%)
    reduce_scatter x2, waiting for transfers between devices, weight_grads(): lax.psum_scatter(jnp.concatenate([contract_rows(shifted, grad_pre), contr...  187 us
    psum x1, waiting for transfers between devices, weight_grads(): total = lax.psum(share, ('dp', 'tx')).astype(jnp.float32)  132 us
    ppermute x4, waiting for transfers between devices, shifted_2(): lax.ppermute(value, axis, [(source, source + steps) for source in range(l...  34.9 us
    dot_general x6, matrix products, mult_trans(): lax.dot_general(left, right, (((1,), (1,)), ((), ())), preferred_element_...  21.2 us
    ppermute x4, starting transfers between devices, shifted_2(): lax.ppermute(value, axis, [(source, source + steps) for source in range(l...  12.9 us
    dot_general x6, matrix products, contract_rows(): lax.dot_general(left, right, (((0,), (0,)), ((), ())), preferred_element_...  12.2 us
    concatenate x2, other arithmetic, weight_grads(): jnp.concatenate([contract_rows(shifted, grad_pre), contract_rows(input_fr...  11.3 us
  transfers between devices with their start and end apart: 7, of which 6 were waited for; matrix products, arithmetic and copies ran while one was open for 9% of the time, Pallas kernels for 0%

commit v1 on v0

--- a/solution.py
+++ b/solution.py
@@ -1,6 +1,8 @@
 import jax
 import jax.numpy as jnp
 from jax import lax
+from jax.experimental import pallas as pl
+from jax.experimental.pallas import tpu as pltpu
 from jax.sharding import PartitionSpec as P
 
 NEAR_DILATION = 64
@@ -78,27 +80,299 @@
     return (grad_in, grad_pre)
 
 
-def weight_grads(shifted, input_frames, grad_pre, gated, grad_out):
-    frame_rows = input_frames.shape[0]
-    width = input_frames.shape[1]
-    streams = lax.axis_size("dp")
-    scale = float(streams * lax.axis_size(("tx", "ty")) * frame_rows) ** (-0.5)
-    share = lax.psum_scatter(
-        jnp.concatenate(
-            [
-                contract_rows(shifted, grad_pre),
-                contract_rows(input_frames, grad_pre),
-                contract_rows(gated, grad_out),
-            ],
-            1,
-        ).astype(jnp.bfloat16),
-        "ty",
-        scatter_dimension=0,
-        tiled=True,
-    )
-    total = lax.psum(share, ("dp", "tx")).astype(jnp.float32)
-    total = total * scale
-    return (total[:, : 4 * width], total[:, 4 * width :])
+MESH = pl.DeviceIdType.MESH
+UNIT = 16
+HALF = 2560
+WIDTHS = ((4, 4, 3, 3, 3, 3), (3, 3, 4, 4, 3, 3))
+
+
+def color_bounds(block):
+    edges = [0]
+    for width in WIDTHS[block]:
+        edges.append(edges[-1] + 128 * width)
+    return [(edges[i], edges[i + 1]) for i in range(6)]
+
+
+def place():
+    dp, tx, ty = (lax.axis_index(name) for name in ("dp", "tx", "ty"))
+    y_hi, core = lax.div(dp, 2), lax.rem(dp, 2)
+    y_lo, z = lax.div(ty, 4), lax.rem(ty, 4)
+    zh, xh = lax.div(z, 2), lax.div(tx, 2)
+    bits = (
+        zh,
+        lax.rem(zh + z, 2),
+        y_hi,
+        lax.rem(y_hi + y_lo, 2),
+        xh,
+        lax.rem(xh + tx, 2),
+    )
+    peers = (
+        {"ty": y_lo * 4 + 3 - z},
+        {"ty": y_lo * 4 + z + 1 - 2 * lax.rem(z, 2)},
+        {"dp": (1 - y_hi) * 2 + core, "ty": (1 - y_lo) * 4 + z},
+        {"ty": (1 - y_lo) * 4 + z},
+        {"tx": 3 - tx},
+        {"tx": tx + 1 - 2 * lax.rem(tx, 2)},
+    )
+    other_core = {"dp": y_hi * 2 + 1 - core}
+    far_y = {"dp": (1 - y_hi) * 2 + core}
+    return bits, core, peers, other_core, far_y
+
+
+def order_of(color):
+    return [(color + step) % 6 for step in range(6)]
+
+
+def remote(source, target, send_sem, recv_sem, peer):
+    return pltpu.make_async_remote_copy(
+        src_ref=source,
+        dst_ref=target,
+        send_sem=send_sem,
+        recv_sem=recv_sem,
+        device_id=peer,
+        device_id_type=MESH,
+    )
+
+
+def reduce_kernel(
+    s2, x2, t2, p2, g2, s1, x1, t1, p1, g1, out,
+    lhs_in, pre_in, grad_in, acc, got, full,
+    ex_send, ex_recv, rs_send, rs_recv, ag_send, ag_recv, local_sem,
+):
+    bits, core, peers, other_core, far_y = place()
+    blocks = ((s2, x2, t2, p2, g2), (s1, x1, t1, p1, g1))
+    barrier = pltpu.get_barrier_semaphore()
+    for peer in peers + (other_core, far_y):
+        pl.semaphore_signal(barrier, inc=1, device_id=peer, device_id_type=MESH)
+    pl.semaphore_wait(barrier, 8)
+
+    def half(ref, which, width):
+        return ref.at[:, pl.ds(pl.multiple_of(which * width, width), width)]
+
+    exchange = []
+    for b, (s, x, t, p, g) in enumerate(blocks):
+        pairs = [
+            (s, lhs_in.at[b, 0]),
+            (x, lhs_in.at[b, 1]),
+            (t, lhs_in.at[b, 2]),
+            (half(p, 1 - core, 1024), pre_in.at[b]),
+            (half(g, 1 - core, 512), grad_in.at[b]),
+        ]
+        copies = [
+            remote(a, c, ex_send.at[b, i], ex_recv.at[b, i], other_core)
+            for i, (a, c) in enumerate(pairs)
+        ]
+        for copy in copies:
+            copy.start()
+        exchange.append(copies)
+
+    def weight_products(b):
+        s, x, t, p, g = blocks[b]
+        own_p, own_g = half(p, core, 1024), half(g, core, 512)
+        bounds = color_bounds(b)
+
+        def body(m, carry):
+            start = pl.multiple_of(m * 256, 256)
+            for part, own in enumerate((s, x, t)):
+                left = jnp.concatenate(
+                    [own[:, pl.ds(start, 256)], lhs_in[b, part, :, pl.ds(start, 256)]], 0
+                )
+                for piece in range(2 if part < 2 else 1):
+                    if part < 2:
+                        lo = piece * 512
+                        right = jnp.concatenate(
+                            [own_p[:, lo : lo + 512], pre_in[b, :, lo : lo + 512]], 0
+                        )
+                    else:
+                        lo = 0
+                        right = jnp.concatenate([own_g[...], grad_in[b]], 0)
+                    product = contract_rows(left, right).astype(jnp.bfloat16)
+                    first = part * 1024 + lo
+                    for row in range(16):
+                        ty = 2 * m + row // 8
+                        y_lo, z = lax.div(ty, 4), lax.rem(ty, 4)
+                        zh = lax.div(z, 2)
+                        side = (row // 4) % 2
+                        unit = (
+                            zh,
+                            lax.rem(zh + z, 2),
+                            side,
+                            lax.rem(side + y_lo, 2),
+                            (row // 2) % 2,
+                            row % 2,
+                        )
+                        for color, (begin, end) in enumerate(bounds):
+                            begin, end = max(begin, first), min(end, first + 512)
+                            if begin >= end:
+                                continue
+                            spot = 0
+                            for step, dim in enumerate(order_of(color)):
+                                spot = spot + unit[dim] * 2 ** (5 - step)
+                            acc[b, spot, :, begin:end] = product[
+                                row * 16 : row * 16 + 16, begin - first : end - first
+                            ]
+            return carry
+
+        lax.fori_loop(0, 4, body, 0)
+
+    def ranges(color, step):
+        base = 0
+        for earlier, dim in enumerate(order_of(color)[:step]):
+            base = base + bits[dim] * 2 ** (5 - earlier)
+        count = 2 ** (5 - step)
+        mine = bits[order_of(color)[step]]
+        return base + mine * count, base + (1 - mine) * count, count
+
+    def reduce_copy(b, color, step):
+        begin, end = color_bounds(b)[color]
+        keep, give, count = ranges(color, step)
+        spot = (b, pl.ds(give, count), slice(None), slice(begin, end))
+        landing = (b, pl.ds(keep, count), slice(None), slice(begin, end))
+        return remote(
+            acc.at[spot], got.at[landing], rs_send.at[b, color, step],
+            rs_recv.at[b, color, step], peers[order_of(color)[step]],
+        )
+
+    def arrival(b, color, step):
+        begin, end = color_bounds(b)[color]
+        keep, give, count = ranges(color, step)
+        spot = (b, pl.ds(give, count), slice(None), slice(begin, end))
+        return remote(
+            acc.at[spot], got.at[spot], rs_send.at[b, color, step],
+            rs_recv.at[b, color, step], peers[order_of(color)[step]],
+        )
+
+    def fold(b, color, step):
+        begin, end = color_bounds(b)[color]
+        keep, give, count = ranges(color, step)
+        chunk = min(count, 4)
+
+        def total(i):
+            here = acc[b, pl.ds(keep + i * chunk, chunk), :, begin:end]
+            there = got[b, pl.ds(give + i * chunk, chunk), :, begin:end]
+            sum_ = here.astype(jnp.float32) + there.astype(jnp.float32)
+            return sum_.astype(jnp.bfloat16)
+
+        if step == 5:
+            full[b, core, bits[2], bits[4], bits[5], :, begin:end] = total(0)[0]
+            return
+
+        def body(i, carry):
+            acc[b, pl.ds(keep + i * chunk, chunk), :, begin:end] = total(i)
+            return carry
+
+        lax.fori_loop(0, count // chunk, body, 0)
+
+    for b in range(2):
+        for copy in exchange[b]:
+            copy.wait_recv()
+        weight_products(b)
+        for color in range(6):
+            reduce_copy(b, color, 0).start()
+    for step in range(6):
+        for b in range(2):
+            for color in range(6):
+                arrival(b, color, step).wait_recv()
+                fold(b, color, step)
+                if step < 5:
+                    reduce_copy(b, color, step + 1).start()
+
+    yh, xh, xq = bits[2], bits[4], bits[5]
+    every = slice(None)
+
+    def gather_copy(b, index, where, target):
+        ref = full.at[(b, core) + where]
+        return remote(ref, ref, ag_send.at[b, index], ag_recv.at[b, index], target)
+
+    left, right = slice(0, HALF // 2), slice(HALF // 2, HALF)
+
+    def first_copies(b):
+        return [
+            gather_copy(b, 1, (every, xh, xq, every, left), peers[5]),
+            gather_copy(b, 2, (every, xh, xq, every, right), peers[4]),
+        ]
+
+    def second_copies(b):
+        return [
+            gather_copy(b, 3, (every, xh, every, every, left), peers[4]),
+            gather_copy(b, 4, (every, every, xq, every, right), peers[5]),
+        ]
+
+    gathered = [[], []]
+    for b in range(2):
+        copy = gather_copy(b, 0, (yh, xh, xq), far_y)
+        copy.start()
+        gathered[b].append(copy)
+    for b in range(2):
+        gathered[b][0].wait_recv()
+        for copy in first_copies(b):
+            copy.start()
+            gathered[b].append(copy)
+    for b in range(2):
+        gathered[b][1].wait_recv()
+        gathered[b][2].wait_recv()
+        for copy in second_copies(b):
+            copy.start()
+            gathered[b].append(copy)
+    for b in range(2):
+        gathered[b][3].wait_recv()
+        gathered[b][4].wait_recv()
+        ref = full.at[b, core]
+        copy = remote(ref, ref, ag_send.at[b, 5], ag_recv.at[b, 5], other_core)
+        copy.start()
+        gathered[b].append(copy)
+    for b in range(2):
+        gathered[b][5].wait_recv()
+        store = pltpu.make_async_copy(full.at[b], out.at[b], local_sem.at[b])
+        store.start()
+    for b in range(2):
+        for copy in exchange[b] + gathered[b]:
+            copy.wait_send()
+        for color in range(6):
+            for step in range(6):
+                reduce_copy(b, color, step).wait_send()
+        pltpu.make_async_copy(full.at[b], out.at[b], local_sem.at[b]).wait()
+
+
+def weight_totals(*operands):
+    vmem = pl.BlockSpec(memory_space=pltpu.VMEM)
+    shape = (2, 2, 2, 2, 2, UNIT, HALF)
+    return pl.pallas_call(
+        reduce_kernel,
+        out_shape=jax.ShapeDtypeStruct(shape, jnp.bfloat16),
+        in_specs=[vmem] * 10,
+        out_specs=pl.BlockSpec(memory_space=pl.ANY),
+        scratch_shapes=[
+            pltpu.VMEM((2, 3, 384, 1024), jnp.bfloat16),
+            pltpu.VMEM((2, 384, 1024), jnp.bfloat16),
+            pltpu.VMEM((2, 384, 512), jnp.bfloat16),
+            pltpu.VMEM((2, 64, UNIT, HALF), jnp.bfloat16),
+            pltpu.VMEM((2, 64, UNIT, HALF), jnp.bfloat16),
+            pltpu.VMEM(shape, jnp.bfloat16),
+            pltpu.SemaphoreType.DMA((2, 5)),
+            pltpu.SemaphoreType.DMA((2, 5)),
+            pltpu.SemaphoreType.DMA((2, 6, 6)),
+            pltpu.SemaphoreType.DMA((2, 6, 6)),
+            pltpu.SemaphoreType.DMA((2, 6)),
+            pltpu.SemaphoreType.DMA((2, 6)),
+            pltpu.SemaphoreType.DMA((2,)),
+        ],
+        compiler_params=pltpu.CompilerParams(
+            collective_id=0, has_side_effects=True, vmem_limit_bytes=60 * 2**20
+        ),
+    )(*operands)
+
+
+def scaled(total, rows):
+    scale = float(
+        lax.axis_size("dp") * lax.axis_size(("tx", "ty")) * rows
+    ) ** (-0.5)
+    total = total.reshape(2, 128, HALF)
+    value = total.astype(jnp.float32) * scale
+    conv = jnp.concatenate(
+        [value[0, :, :1024], value[1, :, :1024], value[0, :, 1024:2048], value[1, :, 1024:2048]], 1
+    )
+    return conv, jnp.concatenate([value[0, :, 2048:], value[1, :, 2048:]], 1)
 
 
 def shards(
@@ -127,9 +401,6 @@
         second_residual_projection,
         back_far,
     )
-    conv_two_grad, proj_two_grad = weight_grads(
-        far_input, middle_activation, second_preactivation, second_gated_value, output_gradient
-    )
     input_gradient, first_preactivation = backward_layer_pass(
         first_tanh_filter,
         first_gate,
@@ -138,9 +409,12 @@
         first_residual_projection,
         back_near,
     )
-    conv_one_grad, proj_one_grad = weight_grads(
-        near_input, block_input, first_preactivation, first_gated_value, middle_gradient
-    )
+    totals = weight_totals(
+        far_input, middle_activation, second_gated_value, second_preactivation, output_gradient,
+        near_input, block_input, first_gated_value, first_preactivation, middle_gradient,
+    )
+    conv_two_grad, proj_two_grad = scaled(totals[0], block_input.shape[0])
+    conv_one_grad, proj_one_grad = scaled(totals[1], block_input.shape[0])
     return (
         block_output[None],
         input_gradient[None],

time: 452 us -> 171 us (0.38)
  waiting for transfers between devices: 354 us -> 29.8 us
  Pallas kernels: 0 us -> 89.7 us
  matrix products: 45.9 us -> 24.2 us
  between operations: 14.4 us -> 1.1 us
  local copies, waits for them, and re-layouts: 8.62 us -> 3.12 us
    reduce_scatter x2 -> x0, waiting for transfers between devices: 187 us -> none  [weight_grads(): lax.psum_scatter(jnp.concatenate([contract_rows(shifted, grad_pre), contr...]
    psum x1 -> x0, waiting for transfers between devices: 132 us -> none  [weight_grads(): total = lax.psum(share, ('dp', 'tx')).astype(jnp.float32)]
    pallas_call x0 -> x1, Pallas kernels: none -> 89.7 us  [weight_totals(): pl.pallas_call(reduce_kernel, out_shape=jax.ShapeDtypeStruct(shape, jnp.b...]
    dot_general x6 -> x0, matrix products: 12.2 us -> none  [contract_rows(): lax.dot_general(left, right, (((0,), (0,)), ((), ())), preferred_element_...]
    dot_general x6, matrix products: 21.2 us -> 11.6 us  [mult_trans(): lax.dot_general(left, right, (((1,), (1,)), ((), ())), preferred_element_...]
    ppermute x4, waiting for transfers between devices: 34.9 us -> 29.8 us  [shifted_2(): lax.ppermute(value, axis, [(source, source + steps) for source in range(l...]
    slice x4 -> x0, local copies, waits for them, and re-layouts: 4.63 us -> none  [weight_grads(): return (total[:, :4 * width], total[:, 4 * width:])]
    concatenate x2 -> x5, other arithmetic: 11.3 us -> 7.17 us  [the longest x2 2.63 us: backward_layer_pass(): jnp.concatenate([grad_gated * gate_part * (1.0 - tanh_part * tanh_part),...]
  transfers between devices with their start and end apart: 7 -> 4, of which waited for: 6 -> 3; matrix products, arithmetic and copies ran while one was open for 9% -> 8% of each run, Pallas kernels for 0% -> 0%
where the time goes in v1:
time: 171 us
  Pallas kernels  89.7 us (52%)
  waiting for transfers between devices  29.8 us (17%)
  matrix products  24.2 us (14%)
  starting transfers between devices  12.4 us (7%)
  other arithmetic  10.4 us (6%)
  local copies, waits for them, and re-layouts  3.12 us (2%)
    pallas_call x1, Pallas kernels, weight_totals(): pl.pallas_call(reduce_kernel, out_shape=jax.ShapeDtypeStruct(shape, jnp.b...  89.7 us
    ppermute x4, waiting for transfers between devices, shifted_2(): lax.ppermute(value, axis, [(source, source + steps) for source in range(l...  29.8 us
    ppermute x4, starting transfers between devices, shifted_2(): lax.ppermute(value, axis, [(source, source + steps) for source in range(l...  12.4 us
    dot_general x6, matrix products, mult_trans(): lax.dot_general(left, right, (((1,), (1,)), ((), ())), preferred_element_...  11.6 us
    dot_general x2, matrix products, causal_parts(): jnp.dot(input_frames, conv_weight[:, 2 * width:], preferred_element_type=...  6.05 us
    dot_general x2, matrix products, causal_parts(): jnp.dot(shifted, conv_weight[:, :2 * width], preferred_element_type=jnp.f...  3.67 us
  transfers between devices with their start and end apart: 4, of which 3 were waited for; matrix products, arithmetic and copies ran while one was open for 8% of the time, Pallas kernels for 0%

profile of v1, /device:TPU:1, one launch (start us, length us, event | category | flops | bytes accessed | tf_op | source)
XLA Modules:
  0.0 170.7 jit_solution(10016663321535407765)
XLA Ops:
  0.6 0.0 copy-start
  0.6 1.1 slice_bitcast_fusion.13
  1.7 4.6 %collective-permute-start = (bf16[64,1024]{1,0:T(8,128)(2,1)S(1)}, bf16[64,1024]{1,0:T(8,128)(2,1)S(1)}, u32[]{:S(2)}, u32[]{:S(2)}) collective-permute-start(bf16[64,1024]{1,0:T(8,128)(2,1)S(1)} %slice_bitcast_fusion.13), channel_id=1, source_target_pairs={{0,1},{1,2},{2,3},{3,4},{4,5},{5,6},{6,7},{7,8},{8,9},{9,10},{10,1... | collective-permute-start | bytes 393224 | tf_op jit(solution)/shard_map/ppermute | solution.py:14
  6.4 4.2 %fusion.10 = f32[384,2048]{1,0:T(8,128)S(1)} fusion(bf16[1024,4096]{1,0:T(8,128)(2,1)} %param.7, bf16[1,384,1024]{2,1,0:T(8,128)(2,1)} %param.6), kind=kOutput, calls=%fused_computation.10 | convolution fusion | flops 1610612736 | bytes 8126464 | tf_op jit(solution)/shard_map/dot_general | solution.py:53
  10.7 1.8 %fusion.16 = f32[384,2048]{1,0:T(8,128)S(1)} fusion(f32[384,2048]{1,0:T(8,128)S(1)} %fusion.10, bf16[1024,4096]{1,0:T(8,128)(2,1)S(1)} %copy-done.15, bf16[320,1024]{1,0:T(8,128)(2,1)S(1)} %slice_bitcast_fusion, bf16[64,1024]{1,0:T(8,128)(2,1)S(1)} %collective-permute-done), kind=kOutput, calls=%fused_computation.16 | convolution fusion | flops 1612972032 | bytes 11272192 | tf_op jit(solution)/shard_map/dot_general | solution.py:52
  12.6 0.6 multiply_convert_fusion.5.t1
  13.2 1.4 copy-done.16
  14.7 1.0 add_convert_fusion.3.x2
  15.7 4.7 %collective-permute-start.1 = (bf16[384,1024]{1,0:T(8,128)(2,1)S(1)}, bf16[384,1024]{1,0:T(8,128)(2,1)S(1)}, u32[]{:S(2)}, u32[]{:S(2)}) collective-permute-start(bf16[384,1024]{1,0:T(8,128)(2,1)S(1)} %add_convert_fusion.3.x2), channel_id=1, source_target_pairs={{0,8},{1,9},{2,10},{3,11},{4,12},{5,13},{6,14},{7,15},{8,16},{9,17... | collective-permute-start | bytes 2359304 | tf_op jit(solution)/shard_map/ppermute | solution.py:14
  20.5 1.8 %fusion.2 = f32[384,2048]{1,0:T(8,128)S(1)} fusion(bf16[384,1024]{1,0:T(8,128)(2,1)S(1)} %add_convert_fusion.3.x2, bf16[1024,4096]{1,0:T(8,128)(2,1)S(1)} %bitcast.60), kind=kOutput, calls=%fused_computation.2 | convolution fusion | flops 1610612736 | bytes 8126464 | tf_op jit(solution)/shard_map/dot_general | solution.py:53
  22.3 13.7 %collective-permute-done.1.s2 = bf16[384,1024]{1,0:T(8,128)(2,1)S(1)} collective-permute-done((bf16[384,1024]{1,0:T(8,128)(2,1)S(1)}, bf16[384,1024]{1,0:T(8,128)(2,1)S(1)}, u32[]{:S(2)}, u32[]{:S(2)}) %collective-permute-start.1) | collective-permute-done | bytes 786464 | tf_op jit(solution)/shard_map/ppermute | solution.py:14
  36.0 1.8 %fusion.19 = f32[384,2048]{1,0:T(8,128)S(1)} fusion(f32[384,2048]{1,0:T(8,128)S(1)} %fusion.2, bf16[384,1024]{1,0:T(8,128)(2,1)S(1)} %collective-permute-done.1.s2, bf16[1024,4096]{1,0:T(8,128)(2,1)S(1)} %bitcast.60), kind=kOutput, calls=%fused_computation.17 | convolution fusion | flops 1611399168 | bytes 11272192 | tf_op jit(solution)/shard_map/dot_general | solution.py:52
  37.9 1.7 multiply_convert_fusion.3
  39.6 1.8 %fusion.33 = bf16[384,1024]{1,0:T(8,128)(2,1)S(1)} fusion(bf16[1024,4096]{1,0:T(8,128)(2,1)S(1)} %bitcast.60, bf16[384,1024]{1,0:T(8,128)(2,1)S(1)} %get-tuple-element.9, bf16[384,1024]{1,0:T(8,128)(2,1)S(1)} %get-tuple-element.8), kind=kOutput, calls=%fused_computation.45 | convolution fusion | flops 1614151680 | bytes 6553600 | tf_op jit(solution)/shard_map/dot_general | solution.py:18
  41.4 1.5 collective-permute-start.2
  42.9 1.0 pad_maximum_fusion.4.s1
  43.9 1.3 pad_maximum_fusion.2.p2
  45.2 1.9 %fusion.36 = bf16[1,384,1024]{2,1,0:T(8,128)(2,1)} fusion(bf16[384,1024]{1,0:T(8,128)(2,1)S(1)} %get-tuple-element.10.t2, bf16[1024,1024]{1,0:T(8,128)(2,1)S(1)} %copy-done, bf16[384,1024]{1,0:T(8,128)(2,1)S(1)} %add_convert_fusion.3.x2), kind=kOutput, calls=%fused_computation.46 | convolution fusion | flops 806486016 | bytes 4456448 | tf_op jit(solution)/shard_map/dot_general | solution.py:61
  47.1 14.3 %collective-permute-done.2 = bf16[384,1024]{1,0:T(8,128)(2,1)S(1)} collective-permute-done((bf16[384,1024]{1,0:T(8,128)(2,1)S(1)}, bf16[384,1024]{1,0:T(8,128)(2,1)S(1)}, u32[]{:S(2)}, u32[]{:S(2)}) %collective-permute-start.2) | collective-permute-done | bytes 786464 | tf_op jit(solution)/shard_map/ppermute | solution.py:14
  61.3 1.9 %add_convert_fusion.1.g1 = bf16[384,1024]{1,0:T(8,128)(2,1)S(1)} fusion(bf16[384,1024]{1,0:T(8,128)(2,1)S(1)} %collective-permute-done.2, bf16[1024,4096]{1,0:T(8,128)(2,1)S(1)} %bitcast.60, bf16[1,384,1024]{2,1,0:T(8,128)(2,1)S(1)} %copy-done.4, bf16[384,1024]{1,0:T(8,128)(2,1)S(1)} %get-tuple-element.9, bf16[384,1024]{1,0:T(8,128)(2,1)S(1)} %get-tuple-element.8), kind=kOutput, calls=%fused_computation.37 | convolution fusion | flops 1615724544 | bytes 8126464 | tf_op jit(solution)/shard_map/dot_general | solution.py:18
  63.3 1.5 multiply_convert_fusion.1
  64.8 1.9 %fusion.30 = bf16[384,1024]{1,0:T(8,128)(2,1)S(1)} fusion(bf16[1024,4096]{1,0:T(8,128)(2,1)S(1)} %copy-done.15, bf16[384,1024]{1,0:T(8,128)(2,1)S(1)} %get-tuple-element.7, bf16[384,1024]{1,0:T(8,128)(2,1)S(1)} %get-tuple-element.6), kind=kOutput, calls=%fused_computation.44 | convolution fusion | flops 1614151680 | bytes 6553600 | tf_op jit(solution)/shard_map/dot_general | solution.py:18
  66.8 1.4 pad_maximum_fusion.3.p1
  68.1 89.7 %shard_map.109 = bf16[2,2,2,2,2,16,2560]{6,5,4,3,2,1,0:T(8,128)(2,1)} custom-call(bf16[384,1024]{1,0:T(8,128)(2,1)} %copy-done.8, bf16[384,1024]{1,0:T(8,128)(2,1)} %copy-done.7, bf16[384,1024]{1,0:T(8,128)(2,1)} %copy-done.9, bf16[384,2048]{1,0:T(8,128)(2,1)} %pad_maximum_fusion.2.p2, bf16[384,1024]{1,0:T(8,128)(2,1)} %bitcast.58, ...), custom_call_target="tpu_custom_call" | custom-call | tf_op jit(solution)/shard_map/pallas_call | solution.py:340
  157.9 2.6 %convert_multiply_fusion = (f32[1,2,2,2,2,16,2560]{6,5,4,3,2,1,0:T(8,128)S(1)}, f32[1,2,2,2,2,16,2560]{6,5,4,3,2,1,0:T(8,128)S(1)}) fusion(bf16[2,2,2,2,2,16,2560]{6,5,4,3,2,1,0:T(8,128)(2,1)} %shard_map.109), kind=kLoop, calls=%fused_computation.18 | loop fusion | flops 2621440 | bytes 7864320 | tf_op jit(solution)/shard_map/mul | solution.py:371
  160.5 0.2 slice_bitcast_fusion.8
  160.8 0.2 slice_bitcast_fusion.4
  160.9 1.6 collective-permute-start.3
  162.5 2.5 %pad_maximum_fusion = (f32[128,4096]{1,0:T(8,128)}, f32[128,4096]{1,0:T(8,128)}) fusion(f32[128,1024]{1,0:T(8,128)S(1)} %get-tuple-element.22, f32[128,1024]{1,0:T(8,128)S(1)} %get-tuple-element.23, f32[128,1024]{1,0:T(8,128)S(1)} %get-tuple-element.24, f32[128,1024]{1,0:T(8,128)S(1)} %get-tuple-element.21, f32[128,1024]{1,0:T(8,128)S(1)} %get-tuple-element.14, ...), kind=kLoop, calls=%fused_computation.20 | loop fusion | flops 3145728 | bytes 8388608 | tf_op jit(solution)/shard_map/concatenate | solution.py:372
  165.0 1.1 pad_maximum_fusion.5
  166.0 1.9 %collective-permute-done.3 = bf16[64,1024]{1,0:T(8,128)(2,1)S(1)} collective-permute-done((bf16[64,1024]{1,0:T(8,128)(2,1)S(1)}, bf16[64,1024]{1,0:T(8,128)(2,1)S(1)}, u32[]{:S(2)}, u32[]{:S(2)}) %collective-permute-start.3) | collective-permute-done | bytes 131104 | tf_op jit(solution)/shard_map/ppermute | solution.py:14
  168.0 2.8 %fusion.37 = bf16[1,384,1024]{2,1,0:T(8,128)(2,1)} fusion(bf16[384,1024]{1,0:T(8,128)(2,1)S(1)} %copy-done.6, bf16[64,1024]{1,0:T(8,128)(2,1)S(1)} %collective-permute-done.3, bf16[320,1024]{1,0:T(8,128)(2,1)S(1)} %slice-done, bf16[1024,4096]{1,0:T(8,128)(2,1)S(1)} %bitcast.62, bf16[384,1024]{1,0:T(8,128)(2,1)S(1)} %copy-done.14, ...), kind=kOutput, calls=%fused_computation.47 | convolution fusion | flops 1616904192 | bytes 8126464 | tf_op jit(solution)/shard_map/dot_general | solution.py:18
  (49 shorter events, 0.2 us)
Async XLA Ops:
  0.6 37.3 %copy-start = (bf16[1024,1024]{1,0:T(8,128)(2,1)S(1)}, bf16[1024,1024]{1,0:T(8,128)(2,1)}, u32[]{:S(2)}) copy-start(bf16[1024,1024]{1,0:T(8,128)(2,1)} %param.10) | copy-start | bytes 6291460
  1.7 8.9 %copy-start.2 = (bf16[1,384,1024]{2,1,0:T(8,128)(2,1)S(1)}, bf16[1,384,1024]{2,1,0:T(8,128)(2,1)}, u32[]{:S(2)}) copy-start(bf16[1,384,1024]{2,1,0:T(8,128)(2,1)} %param.6) | copy-start | bytes 2359300
  1.7 9.0 %copy-start.15 = (bf16[1024,4096]{1,0:T(8,128)(2,1)S(1)}, bf16[1024,4096]{1,0:T(8,128)(2,1)}, u32[]{:S(2)}) copy-start(bf16[1024,4096]{1,0:T(8,128)(2,1)} %param.7) | copy-start | bytes 25165828
  1.7 9.0 %collective-permute-start = (bf16[64,1024]{1,0:T(8,128)(2,1)S(1)}, bf16[64,1024]{1,0:T(8,128)(2,1)S(1)}, u32[]{:S(2)}, u32[]{:S(2)}) collective-permute-start(bf16[64,1024]{1,0:T(8,128)(2,1)S(1)} %slice_bitcast_fusion.13), channel_id=1, source_target_pairs={{0,1},{1,2},{2,3},{3,4},{4,5},{5,6},{6,7},{7,8},{8,9},{9,10},{10,1... | collective-permute-start | bytes 393224 | tf_op jit(solution)/shard_map/ppermute | solution.py:14
  10.6 9.8 %slice-start.1 = ((s8[8388608]{0:T(1024)(128)(4,1)}), s8[4194304]{0:T(1024)(128)(4,1)S(1)}, s32[]{:S(2)}) async-start(s8[8388608]{0:T(1024)(128)(4,1)} %bitcast.59), calls=%async_computation.1 | async-start | bytes 8388608
  10.7 9.8 %slice-start.2 = ((s8[8388608]{0:T(1024)(128)(4,1)}), s8[4194304]{0:T(1024)(128)(4,1)S(1)}, s32[]{:S(2)}) async-start(s8[8388608]{0:T(1024)(128)(4,1)} %bitcast.59), calls=%async_computation.2 | async-start | bytes 8388608
  12.6 2.1 %copy-start.16 = (bf16[1024,1024]{1,0:T(8,128)(2,1)S(1)}, bf16[1024,1024]{1,0:T(8,128)(2,1)}, u32[]{:S(2)}) copy-start(bf16[1024,1024]{1,0:T(8,128)(2,1)} %param.8) | copy-start | bytes 6291460
  14.7 1.0 copy-start.3
  15.7 29.5 %copy-start.7 = (bf16[384,1024]{1,0:T(8,128)(2,1)}, bf16[384,1024]{1,0:T(8,128)(2,1)S(1)}, u32[]{:S(2)}) copy-start(bf16[384,1024]{1,0:T(8,128)(2,1)S(1)} %add_convert_fusion.3.x2) | copy-start | bytes 2359300
  15.7 20.3 %collective-permute-start.1 = (bf16[384,1024]{1,0:T(8,128)(2,1)S(1)}, bf16[384,1024]{1,0:T(8,128)(2,1)S(1)}, u32[]{:S(2)}, u32[]{:S(2)}) collective-permute-start(bf16[384,1024]{1,0:T(8,128)(2,1)S(1)} %add_convert_fusion.3.x2), channel_id=1, source_target_pairs={{0,8},{1,9},{2,10},{3,11},{4,12},{5,13},{6,14},{7,15},{8,16},{9,17... | collective-permute-start | bytes 2359304 | tf_op jit(solution)/shard_map/ppermute | solution.py:14
  22.3 15.6 %copy-start.4 = (bf16[1,384,1024]{2,1,0:T(8,128)(2,1)S(1)}, bf16[1,384,1024]{2,1,0:T(8,128)(2,1)}, u32[]{:S(2)}) copy-start(bf16[1,384,1024]{2,1,0:T(8,128)(2,1)} %param.11) | copy-start | bytes 2359300
  36.0 1.8 %copy-start.8 = (bf16[384,1024]{1,0:T(8,128)(2,1)}, bf16[384,1024]{1,0:T(8,128)(2,1)S(1)}, u32[]{:S(2)}) copy-start(bf16[384,1024]{1,0:T(8,128)(2,1)S(1)} %collective-permute-done.1.s2) | copy-start | bytes 2359300
  39.6 5.6 %copy-start.9 = (bf16[384,1024]{1,0:T(8,128)(2,1)}, bf16[384,1024]{1,0:T(8,128)(2,1)S(1)}, u32[]{:S(2)}) copy-start(bf16[384,1024]{1,0:T(8,128)(2,1)S(1)} %get-tuple-element.10.t2) | copy-start | bytes 2359300
  41.4 19.9 %collective-permute-start.2 = (bf16[384,1024]{1,0:T(8,128)(2,1)S(1)}, bf16[384,1024]{1,0:T(8,128)(2,1)S(1)}, u32[]{:S(2)}, u32[]{:S(2)}) collective-permute-start(bf16[384,1024]{1,0:T(8,128)(2,1)S(1)} %fusion.33), channel_id=1, source_target_pairs={{8,0},{9,1},{10,2},{11,3},{12,4},{13,5},{14,6},{15,7},{16,8},{17,9... | collective-permute-start | bytes 2359304 | tf_op jit(solution)/shard_map/ppermute | solution.py:14
  63.2 1.5 copy-start.5
  64.8 1.9 %copy-start.11 = (bf16[384,1024]{1,0:T(8,128)(2,1)}, bf16[384,1024]{1,0:T(8,128)(2,1)S(1)}, u32[]{:S(2)}) copy-start(bf16[384,1024]{1,0:T(8,128)(2,1)S(1)} %get-tuple-element.6) | copy-start | bytes 2359300
  64.8 1.9 %copy-start.13 = (bf16[384,1024]{1,0:T(8,128)(2,1)}, bf16[384,1024]{1,0:T(8,128)(2,1)S(1)}, u32[]{:S(2)}) copy-start(bf16[384,1024]{1,0:T(8,128)(2,1)S(1)} %get-tuple-element.7) | copy-start | bytes 2359300
  66.7 1.4 copy-start.10
  157.9 10.0 %slice-start.3 = ((s8[8388608]{0:T(1024)(128)(4,1)}), s8[4194304]{0:T(1024)(128)(4,1)S(1)}, s32[]{:S(2)}) async-start(s8[8388608]{0:T(1024)(128)(4,1)} %bitcast.61), calls=%async_computation.3 | async-start | bytes 8388608
  160.7 7.2 %slice-start.4 = ((s8[8388608]{0:T(1024)(128)(4,1)}), s8[4194304]{0:T(1024)(128)(4,1)S(1)}, s32[]{:S(2)}) async-start(s8[8388608]{0:T(1024)(128)(4,1)} %bitcast.61), calls=%async_computation.4 | async-start | bytes 8388608
  160.9 7.0 %collective-permute-start.3 = (bf16[64,1024]{1,0:T(8,128)(2,1)S(1)}, bf16[64,1024]{1,0:T(8,128)(2,1)S(1)}, u32[]{:S(2)}, u32[]{:S(2)}) collective-permute-start(bf16[64,1024]{1,0:T(8,128)(2,1)S(1)} %slice.121), channel_id=1, source_target_pairs={{1,0},{2,1},{3,2},{4,3},{5,4},{6,5},{7,6},{8,7},{9,8},{10,9},{11,1... | collective-permute-start | bytes 393224 | tf_op jit(solution)/shard_map/ppermute | solution.py:14
  162.5 5.4 %copy-start.12 = (bf16[384,1024]{1,0:T(8,128)(2,1)S(1)}, bf16[384,1024]{1,0:T(8,128)(2,1)}, u32[]{:S(2)}) copy-start(bf16[384,1024]{1,0:T(8,128)(2,1)} %copy-done.11) | copy-start | bytes 2359300
  162.5 5.4 %copy-start.14 = (bf16[384,1024]{1,0:T(8,128)(2,1)S(1)}, bf16[384,1024]{1,0:T(8,128)(2,1)}, u32[]{:S(2)}) copy-start(bf16[384,1024]{1,0:T(8,128)(2,1)} %copy-done.13) | copy-start | bytes 2359300
  165.0 2.9 %copy-start.6 = (bf16[384,1024]{1,0:T(8,128)(2,1)S(1)}, bf16[384,1024]{1,0:T(8,128)(2,1)}, u32[]{:S(2)}) copy-start(bf16[384,1024]{1,0:T(8,128)(2,1)} %copy-done.5) | copy-start | bytes 2359300
  165.0 2.9 %slice-start = ((bf16[384,1024]{1,0:T(8,128)(2,1)}), bf16[320,1024]{1,0:T(8,128)(2,1)S(1)}, s32[]{:S(2)}) async-start(bf16[384,1024]{1,0:T(8,128)(2,1)} %copy-done.10), calls=%async_computation | async-start | bytes 1310720 | tf_op jit(solution)/shard_map/slice | solution.py:42
  167.9 2.8 %copy-start.1 = (bf16[1024,1024]{1,0:T(8,128)(2,1)S(1)}, bf16[1024,1024]{1,0:T(8,128)(2,1)}, u32[]{:S(2)}) copy-start(bf16[1024,1024]{1,0:T(8,128)(2,1)} %param.10) | copy-start | bytes 6291460

commit v2 on v0

v2 whole, which is shorter than its diff:
```python
import jax
import jax.numpy as jnp
from jax import lax
from jax.experimental import pallas as pl
from jax.experimental.pallas import tpu as pltpu
from jax.sharding import PartitionSpec as P

NEAR = 64
ROWS = 384
WIDTH = 1024
CHUNKS = 2
CHUNK = ROWS // CHUNKS
TILE = 256

MESH = pl.DeviceIdType.MESH
UNIT = 16
HALF = 2560
WIDTHS = ((4, 4, 3, 3, 3, 3), (3, 3, 4, 4, 3, 3))


def color_bounds(block):
    edges = [0]
    for width in WIDTHS[block]:
        edges.append(edges[-1] + 128 * width)
    return [(edges[i], edges[i + 1]) for i in range(6)]


def place():
    dp, tx, ty = (lax.axis_index(name) for name in ("dp", "tx", "ty"))
    y_hi, core = lax.div(dp, 2), lax.rem(dp, 2)
    y_lo, z = lax.div(ty, 4), lax.rem(ty, 4)
    zh, xh = lax.div(z, 2), lax.div(tx, 2)
    bits = (
        zh,
        lax.rem(zh + z, 2),
        y_hi,
        lax.rem(y_hi + y_lo, 2),
        xh,
        lax.rem(xh + tx, 2),
    )
    peers = (
        {"ty": y_lo * 4 + 3 - z},
        {"ty": y_lo * 4 + z + 1 - 2 * lax.rem(z, 2)},
        {"dp": (1 - y_hi) * 2 + core, "ty": (1 - y_lo) * 4 + z},
        {"ty": (1 - y_lo) * 4 + z},
        {"tx": 3 - tx},
        {"tx": tx + 1 - 2 * lax.rem(tx, 2)},
    )
    other_core = {"dp": y_hi * 2 + 1 - core}
    far_y = {"dp": (1 - y_hi) * 2 + core}
    return bits, core, peers, other_core, far_y


def order_of(color):
    return [(color + step) % 6 for step in range(6)]


def remote(source, target, send_sem, recv_sem, peer):
    return pltpu.make_async_remote_copy(
        src_ref=source,
        dst_ref=target,
        send_sem=send_sem,
        recv_sem=recv_sem,
        device_id=peer,
        device_id_type=MESH,
    )


def dot_nn(left, right):
    return jnp.dot(left, right, preferred_element_type=jnp.float32)


def dot_nt(left, right):
    return lax.dot_general(
        left, right, (((1,), (1,)), ((), ())), preferred_element_type=jnp.float32
    )


def dot_tn(left, right):
    return lax.dot_general(
        left, right, (((0,), (0,)), ((), ())), preferred_element_type=jnp.float32
    )


def step_kernel(
    frames, conv_1, proj_1, conv_2, proj_2, out_grad,
    out_frames, frame_grad, totals,
    w1, w2, q1, q2, xs, mid, s2, t1, t2, g, gmid, gp1, gp2, slope_t, slope_g,
    tap_in, tap_out, near_tap, pre2, wide,
    xs_in, mid_in, s2_in, t1_in, t2_in, gp2_in, g_in, gp1_in, gm_in,
    acc2, got2, got1, full,
    ld_sem, near_send, near_recv, far_send, far_recv, ex_send, ex_recv,
    rs_send, rs_recv, ag_send, ag_recv, st_sem,
):
    bf16, f32 = jnp.bfloat16, jnp.float32
    bits, core, peers, other_core, far_y = place()
    tx, ty = lax.axis_index("tx"), lax.axis_index("ty")
    index = tx * 8 + ty
    after, before = lax.rem(index + 1, 32), lax.rem(index + 31, 32)
    next_peer = {"tx": lax.div(after, 8), "ty": lax.rem(after, 8)}
    prev_peer = {"tx": lax.div(before, 8), "ty": lax.rem(before, 8)}
    later_peer = {"tx": lax.rem(tx + 1, 4)}
    earlier_peer = {"tx": lax.rem(tx + 3, 4)}
    first_shard, last_shard = index == 0, index == 31

    def load(index, source, target):
        return pltpu.make_async_copy(source, target, ld_sem.at[index])

    def columns(start):
        return pl.ds(pl.multiple_of(start, TILE), TILE)

    def conv_loads(j):
        return [
            load(
                4 * j + part,
                conv_1.at[:, pl.ds(part * WIDTH + j * TILE, TILE)],
                w1.at[:, pl.ds(part * WIDTH + j * TILE, TILE)],
            )
            for part in range(4)
        ]

    loads = {"x": load(16, frames.at[0], xs.at[pl.ds(NEAR, ROWS), :])}
    loads["q1"] = load(17, proj_1, q1)
    loads["w2"] = load(18, conv_2, w2)
    loads["g"] = load(19, out_grad.at[0], g)
    loads["q2"] = load(20, proj_2, q2)
    loads["x"].start()
    for j in range(4):
        for copy in conv_loads(j):
            copy.start()
    for name in ("q1", "w2", "g", "q2"):
        loads[name].start()

    barrier = pltpu.get_barrier_semaphore()
    for peer in peers + (other_core, far_y, next_peer, prev_peer):
        pl.semaphore_signal(barrier, inc=1, device_id=peer, device_id_type=MESH)
    pl.semaphore_wait(barrier, 10)

    def half(ref, which, width):
        return ref.at[:, pl.ds(pl.multiple_of(which * width, width), width)]

    def half_rows(ref, which, width, rows):
        return ref.at[rows, pl.ds(pl.multiple_of(which * width, width), width)]

    def swap(item, part, source, target):
        return remote(
            source, target, ex_send.at[item, part], ex_recv.at[item, part], other_core
        )

    every = slice(None)
    top = pl.ds(0, NEAR)
    parts = [pl.ds(c * CHUNK, CHUNK) for c in range(CHUNKS)]
    swaps = {
        "x": [swap(0, 0, frames.at[0], xs_in.at[pl.ds(NEAR, ROWS), :])],
        "halo": [swap(1, 0, xs.at[top, :], xs_in.at[top, :])],
        "g": [swap(2, 0, half(out_grad.at[0], 1 - core, 512), g_in)],
    }
    for item, (name, source, target) in enumerate(
        (("t1", t1, t1_in), ("mid", mid, mid_in), ("s2", s2, s2_in), ("t2", t2, t2_in)), 3
    ):
        swaps[name] = [
            swap(item, c, source.at[rows, :], target.at[rows, :])
            for c, rows in enumerate(parts)
        ]
    for item, (name, source, target, width) in enumerate(
        (("gp2", gp2, gp2_in, 1024), ("gp1", gp1, gp1_in, 1024), ("gm", gmid, gm_in, 512)), 7
    ):
        swaps[name] = [
            swap(item, c, half_rows(source, 1 - core, width, rows), target.at[rows, :])
            for c, rows in enumerate(parts)
        ]

    near_forward = remote(
        frames.at[0, pl.ds(ROWS - NEAR, NEAR), :], xs.at[top, :],
        near_send.at[0], near_recv.at[0], next_peer,
    )
    near_back = remote(
        tap_out.at[top, :], near_tap, near_send.at[1], near_recv.at[1], prev_peer
    )
    far_forward = [
        remote(
            mid.at[rows, :], s2.at[rows, :], far_send.at[0, c], far_recv.at[0, c], later_peer
        )
        for c, rows in enumerate(parts)
    ]
    far_back = [
        remote(
            tap_out.at[rows, :], tap_in.at[rows, :],
            far_send.at[1, c], far_recv.at[1, c], earlier_peer,
        )
        for c, rows in enumerate(parts)
    ]

    near_forward.start()
    swaps["x"][0].start()
    swaps["g"][0].start()
    loads["x"].wait()
    near_forward.wait_recv()

    @pl.when(first_shard)
    def _():
        xs[0:NEAR, :] = jnp.zeros((NEAR, WIDTH), bf16)

    swaps["halo"][0].start()

    def tiles(count, body):
        def step(j, carry):
            body(j)
            return carry

        lax.fori_loop(0, count, step, 0)

    def first_forward(c):
        low = c * CHUNK
        rows = slice(low, low + CHUNK)
        moved = slice(NEAR + low, NEAR + low + CHUNK)

        def gate_tile(j):
            old, now = xs[rows, :], xs[moved, :]
            start = j * TILE
            a = dot_nn(old, w1[:, columns(start)]) + dot_nn(
                now, w1[:, columns(2 * WIDTH + start)]
            )
            v = dot_nn(old, w1[:, columns(WIDTH + start)]) + dot_nn(
                now, w1[:, columns(3 * WIDTH + start)]
            )
            th, gt = jnp.tanh(a), jax.nn.sigmoid(v)
            t1[rows, columns(start)] = (th * gt).astype(bf16)
            slope_t[rows, columns(start)] = (gt * (1.0 - th * th)).astype(bf16)
            slope_g[rows, columns(start)] = (th * gt * (1.0 - gt)).astype(bf16)

        if c == 0:
            for j in range(4):
                for copy in conv_loads(j):
                    copy.wait()
                gate_tile(j)
            loads["q1"].wait()
        else:
            tiles(4, gate_tile)
        swaps["t1"][c].start()

        def out_tile(j):
            value = dot_nn(t1[rows, :], q1[:, columns(j * TILE)])
            value = value + xs[moved, columns(j * TILE)].astype(f32)
            mid[rows, columns(j * TILE)] = value.astype(bf16)

        tiles(4, out_tile)
        far_forward[c].start()
        swaps["mid"][c].start()

    for c in range(CHUNKS):
        first_forward(c)

    loads["w2"].wait()

    def pre_tile(j):
        pre2[:, columns(j * TILE)] = dot_nn(mid[...], w2[:, columns(2 * WIDTH + j * TILE)])

    tiles(8, pre_tile)
    loads["g"].wait()
    loads["q2"].wait()

    def gated_grad_tile(j):
        wide[:, columns(j * TILE)] = dot_nt(g[...], q2[columns(j * TILE), :])

    tiles(4, gated_grad_tile)

    def second_block(c):
        low = c * CHUNK
        rows = slice(low, low + CHUNK)
        far_forward[c].wait_recv()

        @pl.when(tx == 0)
        def _():
            s2[rows, :] = jnp.zeros((CHUNK, WIDTH), bf16)

        swaps["s2"][c].start()

        def gate_tile(j):
            old = s2[rows, :]
            here, there = columns(j * TILE), columns(WIDTH + j * TILE)
            a = dot_nn(old, w2[:, here]) + pre2[rows, here]
            v = dot_nn(old, w2[:, there]) + pre2[rows, there]
            th, gt = jnp.tanh(a), jax.nn.sigmoid(v)
            t2[rows, here] = (th * gt).astype(bf16)
            grad = wide[rows, here] * gt
            gp2[rows, here] = (grad * (1.0 - th * th)).astype(bf16)
            gp2[rows, there] = (grad * th * (1.0 - gt)).astype(bf16)

        tiles(4, gate_tile)
        swaps["t2"][c].start()
        swaps["gp2"][c].start()

        def tap_tile(j):
            value = dot_nt(gp2[rows, :], w2[columns(j * TILE), 0 : 2 * WIDTH])
            tap_out[rows, columns(j * TILE)] = value.astype(bf16)

        tiles(4, tap_tile)
        far_back[c].start()

    for c in range(CHUNKS):
        second_block(c)

    def current_tile(j):
        value = dot_nt(gp2[...], w2[columns(j * TILE), 2 * WIDTH : 4 * WIDTH])
        wide[:, columns(j * TILE)] = value + g[:, columns(j * TILE)].astype(f32)

    tiles(4, current_tile)

    sums, arrivals = (acc2, w2), (got2, got1)

    def weight_products(b):
        if b == 0:
            lefts = ((s2, 0, s2_in), (mid, 0, mid_in), (t2, 0, t2_in))
            own_p, own_g = half(gp2, core, 1024), half(g, core, 512)
            pre_in, grad_in = gp2_in, g_in
        else:
            lefts = ((xs, 0, xs_in), (xs, NEAR, xs_in), (t1, 0, t1_in))
            own_p, own_g = half(gp1, core, 1024), half(gmid, core, 512)
            pre_in, grad_in = gp1_in, gm_in
        bounds = color_bounds(b)

        def product_tile(m):
            for part, (own, low, theirs) in enumerate(lefts):
                span = slice(low, low + ROWS)
                left = jnp.concatenate(
                    [own[span, columns(m * TILE)], theirs[span, columns(m * TILE)]], 0
                )
                for piece in range(2 if part < 2 else 1):
                    lo = piece * 512
                    if part < 2:
                        right = jnp.concatenate(
                            [own_p[:, lo : lo + 512], pre_in[:, lo : lo + 512]], 0
                        )
                    else:
                        right = jnp.concatenate([own_g[...], grad_in[...]], 0)
                    product = dot_tn(left, right).astype(bf16)
                    first = part * 1024 + lo
                    for row in range(16):
                        block = 2 * m + row // 8
                        y_lo, z = lax.div(block, 4), lax.rem(block, 4)
                        zh = lax.div(z, 2)
                        side = (row // 4) % 2
                        unit = (
                            zh,
                            lax.rem(zh + z, 2),
                            side,
                            lax.rem(side + y_lo, 2),
                            (row // 2) % 2,
                            row % 2,
                        )
                        for color, (begin, end) in enumerate(bounds):
                            begin, end = max(begin, first), min(end, first + 512)
                            if begin >= end:
                                continue
                            spot = 0
                            for step, dim in enumerate(order_of(color)):
                                spot = spot + unit[dim] * 2 ** (5 - step)
                            place_rows = pl.ds(pl.multiple_of(spot * UNIT, UNIT), UNIT)
                            sums[b][place_rows, begin:end] = product[
                                row * 16 : row * 16 + 16, begin - first : end - first
                            ]

        tiles(4, product_tile)

    def ranges(color, step):
        base = 0
        for earlier, dim in enumerate(order_of(color)[:step]):
            base = base + bits[dim] * 2 ** (5 - earlier)
        count = 2 ** (5 - step)
        mine = bits[order_of(color)[step]]
        return base + mine * count, base + (1 - mine) * count, count

    def units(start, count):
        return pl.ds(pl.multiple_of(start * UNIT, UNIT), count * UNIT)

    def reduce_copy(b, color, step, landing):
        begin, end = color_bounds(b)[color]
        keep, give, count = ranges(color, step)
        target = keep if landing else give
        return remote(
            sums[b].at[units(give, count), begin:end],
            arrivals[b].at[units(target, count), begin:end],
            rs_send.at[b, color, step], rs_recv.at[b, color, step],
            peers[order_of(color)[step]],
        )

    yh, xh, xq = bits[2], bits[4], bits[5]

    def fold(b, color, step):
        begin, end = color_bounds(b)[color]
        keep, give, count = ranges(color, step)
        chunk = min(count, 4)
        ours, theirs = sums[b], arrivals[b]

        def total(i):
            here = ours[units(keep + i * chunk, chunk), begin:end]
            there = theirs[units(give + i * chunk, chunk), begin:end]
            return (here.astype(f32) + there.astype(f32)).astype(bf16)

        if step == 5:
            full[b, core, yh, xh, xq, :, begin:end] = total(0)
            return

        def put(i):
            ours[units(keep + i * chunk, chunk), begin:end] = total(i)

        tiles(count // chunk, put)

    def advance(b, step):
        for color in range(6):
            reduce_copy(b, color, step, False).wait_recv()
            fold(b, color, step)
            if step < 5:
                reduce_copy(b, color, step + 1, True).start()

    def begin_reduce(b):
        for color in range(6):
            reduce_copy(b, color, 0, True).start()

    for name in ("mid", "s2", "t2", "gp2", "g"):
        for copy in swaps[name]:
            copy.wait_recv()
    weight_products(0)
    begin_reduce(0)

    def first_backward(c):
        low = c * CHUNK
        rows = slice(low, low + CHUNK)
        far_back[c].wait_recv()
        tap = tap_in[rows, :].astype(f32)
        total = wide[rows, :] + jnp.where(tx == 3, 0.0, tap)
        gmid[rows, :] = total.astype(bf16)
        swaps["gm"][c].start()

        def slope_tile(j):
            here, there = columns(j * TILE), columns(WIDTH + j * TILE)
            grad = dot_nt(gmid[rows, :], q1[here, :])
            gp1[rows, here] = (grad * slope_t[rows, here].astype(f32)).astype(bf16)
            gp1[rows, there] = (grad * slope_g[rows, here].astype(f32)).astype(bf16)

        tiles(4, slope_tile)
        swaps["gp1"][c].start()

    for c in range(CHUNKS):
        first_backward(c)
    advance(0, 0)
    for name in ("x", "halo", "t1", "gp1", "gm"):
        for copy in swaps[name]:
            copy.wait_recv()
    weight_products(1)
    begin_reduce(1)
    advance(0, 1)

    for copy in far_back:
        copy.wait_send()

    def first_tap_tile(j):
        value = dot_nt(gp1[...], w1[columns(j * TILE), 0 : 2 * WIDTH])
        tap_out[:, columns(j * TILE)] = value.astype(bf16)

    tiles(4, first_tap_tile)
    near_back.start()
    advance(0, 2)

    def first_current_tile(j):
        value = dot_nt(gp1[...], w1[columns(j * TILE), 2 * WIDTH : 4 * WIDTH])
        pre2[:, columns(j * TILE)] = value + gmid[:, columns(j * TILE)].astype(f32)

    tiles(4, first_current_tile)
    advance(0, 3)
    for copy in far_forward + swaps["mid"]:
        copy.wait_send()

    def second_out_tile(j):
        value = dot_nn(t2[...], q2[:, columns(j * TILE)])
        mid[:, columns(j * TILE)] = (value + mid[:, columns(j * TILE)].astype(f32)).astype(bf16)

    tiles(4, second_out_tile)
    store_out = pltpu.make_async_copy(mid, out_frames.at[0], st_sem.at[0])
    store_out.start()
    advance(1, 0)
    advance(0, 4)
    near_back.wait_recv()
    for copy in swaps["gm"]:
        copy.wait_send()
    body_rows = ROWS - NEAR
    gmid[0:body_rows, :] = (
        pre2[0:body_rows, 0:WIDTH] + tap_out[NEAR:ROWS, :].astype(f32)
    ).astype(bf16)
    edge = jnp.where(last_shard, 0.0, near_tap[...].astype(f32))
    gmid[body_rows:ROWS, :] = (pre2[body_rows:ROWS, 0:WIDTH] + edge).astype(bf16)
    store_grad = pltpu.make_async_copy(gmid, frame_grad.at[0], st_sem.at[1])
    store_grad.start()

    left, right = slice(0, HALF // 2), slice(HALF // 2, HALF)

    def gather_copy(b, index, where, target):
        ref = full.at[(b, core) + where]
        return remote(ref, ref, ag_send.at[b, index], ag_recv.at[b, index], target)

    def gather(b, index):
        if index == 0:
            return gather_copy(b, 0, (yh, xh, xq), far_y)
        if index == 1:
            return gather_copy(b, 1, (every, xh, xq, every, left), peers[5])
        if index == 2:
            return gather_copy(b, 2, (every, xh, xq, every, right), peers[4])
        if index == 3:
            return gather_copy(b, 3, (every, xh, every, every, left), peers[4])
        if index == 4:
            return gather_copy(b, 4, (every, every, xq, every, right), peers[5])
        return gather_copy(b, 5, (), other_core)

    def gather_stage(b, stage):
        waits = ((), (0,), (1, 2), (3, 4), (5,))[stage]
        starts = ((0,), (1, 2), (3, 4), (5,), ())[stage]
        for index in waits:
            gather(b, index).wait_recv()
        for index in starts:
            gather(b, index).start()
        if stage == 4:
            pltpu.make_async_copy(full.at[b], totals.at[b], st_sem.at[2 + b]).start()

    advance(1, 1)
    advance(0, 5)
    gather_stage(0, 0)
    advance(1, 2)
    gather_stage(0, 1)
    advance(1, 3)
    gather_stage(0, 2)
    advance(1, 4)
    gather_stage(0, 3)
    advance(1, 5)
    gather_stage(1, 0)
    gather_stage(0, 4)
    for stage in range(1, 5):
        gather_stage(1, stage)

    near_forward.wait_send()
    near_back.wait_send()
    for name, copies in swaps.items():
        if name not in ("mid", "gm"):
            for copy in copies:
                copy.wait_send()
    for b in range(2):
        for index in range(6):
            gather(b, index).wait_send()
        for color in range(6):
            for step in range(6):
                reduce_copy(b, color, step, True).wait_send()
        pltpu.make_async_copy(full.at[b], totals.at[b], st_sem.at[2 + b]).wait()
    store_out.wait()
    store_grad.wait()


def whole_step(*operands):
    anywhere = pl.BlockSpec(memory_space=pl.ANY)
    bf16, f32 = jnp.bfloat16, jnp.float32
    frame_shape = jax.ShapeDtypeStruct((1, ROWS, WIDTH), bf16)
    totals_shape = (2, 2, 2, 2, 2, UNIT, HALF)
    frame = pltpu.VMEM((ROWS, WIDTH), bf16)
    double = pltpu.VMEM((ROWS, 2 * WIDTH), bf16)
    narrow = pltpu.VMEM((ROWS, WIDTH // 2), bf16)
    weight = pltpu.VMEM((WIDTH, 4 * WIDTH), bf16)
    square = pltpu.VMEM((WIDTH, WIDTH), bf16)
    padded = pltpu.VMEM((ROWS + NEAR, WIDTH), bf16)
    share = pltpu.VMEM((WIDTH, HALF), bf16)
    dma = pltpu.SemaphoreType.DMA
    return pl.pallas_call(
        step_kernel,
        out_shape=[frame_shape, frame_shape, jax.ShapeDtypeStruct(totals_shape, bf16)],
        in_specs=[anywhere] * 6,
        out_specs=[anywhere] * 3,
        scratch_shapes=[
            weight, weight, square, square,
            padded, frame, frame, frame, frame, frame, frame,
            double, double, frame, frame,
            frame, frame, pltpu.VMEM((NEAR, WIDTH), bf16),
            pltpu.VMEM((ROWS, 2 * WIDTH), f32), pltpu.VMEM((ROWS, WIDTH), f32),
            padded, frame, frame, frame, frame, frame, narrow, frame, narrow,
            share, share, share, pltpu.VMEM(totals_shape, bf16),
            dma((21,)), dma((2,)), dma((2,)), dma((2, CHUNKS)), dma((2, CHUNKS)),
            dma((10, CHUNKS)), dma((10, CHUNKS)),
            dma((2, 6, 6)), dma((2, 6, 6)), dma((2, 6)), dma((2, 6)), dma((4,)),
        ],
        compiler_params=pltpu.CompilerParams(
            collective_id=0, has_side_effects=True, vmem_limit_bytes=67043328
        ),
    )(*operands)


def scaled(total, rows):
    scale = float(
        lax.axis_size("dp") * lax.axis_size(("tx", "ty")) * rows
    ) ** (-0.5)
    total = total.reshape(2, 128, HALF)
    value = total.astype(jnp.float32) * scale
    conv = jnp.concatenate(
        [value[0, :, :1024], value[1, :, :1024], value[0, :, 1024:2048], value[1, :, 1024:2048]], 1
    )
    return conv, jnp.concatenate([value[0, :, 2048:], value[1, :, 2048:]], 1)


def shards(*operands):
    block_output, input_gradient, totals = whole_step(*operands)
    conv_two_grad, proj_two_grad = scaled(totals[0], ROWS)
    conv_one_grad, proj_one_grad = scaled(totals[1], ROWS)
    return (
        block_output,
        input_gradient,
        conv_one_grad,
        proj_one_grad,
        conv_two_grad,
        proj_two_grad,
    )


def solution(mesh):
    return jax.shard_map(
        shards,
        mesh=mesh,
        in_specs=(P("dp", ("tx", "ty"), None), P(), P(), P(), P(), P("dp", ("tx", "ty"), None)),
        out_specs=(
            P("dp", ("tx", "ty"), None),
            P("dp", ("tx", "ty"), None),
            P("ty", None),
            P("ty", None),
            P("ty", None),
            P("ty", None),
        ),
        check_vma=False,
    )
```

time: 452 us -> 141 us (0.31)
  waiting for transfers between devices: 354 us -> 0 us
  Pallas kernels: 0 us -> 132 us
  matrix products: 45.9 us -> 0 us
  between operations: 14.4 us -> 0.69 us
  starting transfers between devices: 13.1 us -> 0 us
  other arithmetic: 14.2 us -> 5.95 us
  local copies, waits for them, and re-layouts: 8.62 us -> 2.73 us
    reduce_scatter x2 -> x0, waiting for transfers between devices: 187 us -> none  [weight_grads(): lax.psum_scatter(jnp.concatenate([contract_rows(shifted, grad_pre), contr...]
    psum x1 -> x0, waiting for transfers between devices: 132 us -> none  [weight_grads(): total = lax.psum(share, ('dp', 'tx')).astype(jnp.float32)]
    pallas_call x0 -> x1, Pallas kernels: none -> 132 us  [whole_step(): pl.pallas_call(step_kernel, out_shape=[frame_shape, frame_shape, jax.Shap...]
    dot_general x18 -> x0, matrix products: 45.9 us -> none  [the longest x6 21.2 us: mult_trans(): lax.dot_general(left, right, (((1,), (1,)), ((), ())), preferred_element_...]
    ppermute x4 -> x0, waiting for transfers between devices: 34.9 us -> none  [shifted_2(): lax.ppermute(value, axis, [(source, source + steps) for source in range(l...]
    ppermute x4 -> x0, starting transfers between devices: 12.9 us -> none  [shifted_2(): lax.ppermute(value, axis, [(source, source + steps) for source in range(l...]
    concatenate x2, other arithmetic: 11.3 us -> 3.52 us  [the longest x1 2.46 us: scaled(): jnp.concatenate([value[0, :, :1024], value[1, :, :1024], value[0, :, 1024...]
    slice x8 -> x0, local copies, waits for them, and re-layouts: 5.79 us -> none  [the longest x4 4.63 us: weight_grads(): return (total[:, :4 * width], total[:, 4 * width:])]
  transfers between devices with their start and end apart: 7 -> 0, of which waited for: 6 -> 0; matrix products, arithmetic and copies ran while one was open for 9% -> 0% of each run, Pallas kernels for 0% -> 0%
where the time goes in v2:
time: 141 us
  Pallas kernels  132 us (94%)
  other arithmetic  5.95 us (4%)
  local copies, waits for them, and re-layouts  2.73 us (2%)
    pallas_call x1, Pallas kernels, whole_step(): pl.pallas_call(step_kernel, out_shape=[frame_shape, frame_shape, jax.Shap...  132 us

profile of v2, /device:TPU:1, one launch (start us, length us, event | category | flops | bytes accessed | tf_op | source)
XLA Modules:
  0.0 141.0 jit_solution(7201343896175546176)
XLA Ops:
  0.6 131.7 %shard_map.109 = (bf16[1,384,1024]{2,1,0:T(8,128)(2,1)}, bf16[1,384,1024]{2,1,0:T(8,128)(2,1)}, bf16[2,2,2,2,2,16,2560]{6,5,4,3,2,1,0:T(8,128)(2,1)}) custom-call(bf16[1,384,1024]{2,1,0:T(8,128)(2,1)} %frames.1, bf16[1024,4096]{1,0:T(8,128)(2,1)} %conv_1.1, bf16[1024,1024]{1,0:T(8,128)(2,1)} %proj_1.1, bf16[1024,4096]{1,0:T(8,128)(2,1)} %conv_2.1, ...), custom_call_target="tpu_custom_call" | custom-call | tf_op jit(solution)/shard_map/pallas_call | solution.py:570
  132.3 2.4 %convert_multiply_fusion = (f32[1,2,2,2,2,16,2560]{6,5,4,3,2,1,0:T(8,128)S(1)}, f32[1,2,2,2,2,16,2560]{6,5,4,3,2,1,0:T(8,128)S(1)}) fusion(bf16[2,2,2,2,2,16,2560]{6,5,4,3,2,1,0:T(8,128)(2,1)} %get-tuple-element.11), kind=kLoop, calls=%fused_computation | loop fusion | flops 2621440 | bytes 7864320 | tf_op jit(solution)/shard_map/mul | solution.py:598
  134.8 0.2 slice_bitcast_fusion.7
  135.0 0.2 slice_bitcast_fusion.3
  135.2 1.1 pad_maximum_fusion.2
  136.3 0.0 copy-start.1
  136.3 2.5 %pad_maximum_fusion = (f32[128,4096]{1,0:T(8,128)}, f32[128,4096]{1,0:T(8,128)}) fusion(f32[128,1024]{1,0:T(8,128)S(1)} %get-tuple-element.23, f32[128,1024]{1,0:T(8,128)S(1)} %get-tuple-element.24, f32[128,1024]{1,0:T(8,128)S(1)} %get-tuple-element.25, f32[128,1024]{1,0:T(8,128)S(1)} %get-tuple-element.22, f32[128,1024]{1,0:T(8,128)S(1)} %get-tuple-element.15, ...), kind=kLoop, calls=%fused_computation.2 | loop fusion | flops 3145728 | bytes 8388608 | tf_op jit(solution)/shard_map/concatenate | solution.py:599
  138.7 0.0 copy-start
  138.7 0.0 copy-done.1
  138.7 0.9 copy.14
  139.6 0.5 copy-done
  140.1 0.9 copy.15
  (2 shorter events, 0.1 us)
Async XLA Ops:
  136.3 2.5 %copy-start.1 = (bf16[1,384,1024]{2,1,0:T(8,128)(2,1)S(1)}, bf16[1,384,1024]{2,1,0:T(8,128)(2,1)}, u32[]{:S(2)}) copy-start(bf16[1,384,1024]{2,1,0:T(8,128)(2,1)} %get-tuple-element.36) | copy-start | bytes 2359300
  138.7 1.4 %copy-start = (bf16[1,384,1024]{2,1,0:T(8,128)(2,1)S(1)}, bf16[1,384,1024]{2,1,0:T(8,128)(2,1)}, u32[]{:S(2)}) copy-start(bf16[1,384,1024]{2,1,0:T(8,128)(2,1)} %get-tuple-element.37) | copy-start | bytes 2359300

commit v3 on v2

--- a/solution.py
+++ b/solution.py
@@ -15,14 +15,33 @@
 MESH = pl.DeviceIdType.MESH
 UNIT = 16
 HALF = 2560
-WIDTHS = ((4, 4, 3, 3, 3, 3), (3, 3, 4, 4, 3, 3))
-
-
-def color_bounds(block):
-    edges = [0]
-    for width in WIDTHS[block]:
-        edges.append(edges[-1] + 128 * width)
-    return [(edges[i], edges[i + 1]) for i in range(6)]
+SLABS = 10
+ORDERS = (
+    (
+        (0, 2, 1, 4, 3, 5),
+        (1, 5, 2, 3, 0, 4),
+        (2, 0, 3, 5, 4, 1),
+        (3, 1, 0, 2, 4, 5),
+        (4, 5, 3, 1, 2, 0),
+        (5, 3, 0, 2, 1, 4),
+        (0, 3, 4, 5, 1, 2),
+        (1, 5, 4, 2, 3, 0),
+        (2, 4, 1, 5, 0, 3),
+        (4, 3, 5, 0, 2, 1),
+    ),
+    (
+        (1, 3, 5, 2, 4, 0),
+        (0, 5, 3, 4, 2, 1),
+        (3, 0, 1, 4, 5, 2),
+        (2, 4, 0, 3, 1, 5),
+        (5, 2, 1, 3, 0, 4),
+        (4, 2, 5, 1, 0, 3),
+        (1, 4, 3, 2, 0, 5),
+        (0, 1, 2, 4, 5, 3),
+        (3, 2, 0, 4, 1, 5),
+        (5, 4, 2, 0, 1, 3),
+    ),
+)
 
 
 def place():
@@ -51,10 +70,6 @@
     return bits, core, peers, other_core, far_y
 
 
-def order_of(color):
-    return [(color + step) % 6 for step in range(6)]
-
-
 def remote(source, target, send_sem, recv_sem, peer):
     return pltpu.make_async_remote_copy(
         src_ref=source,
@@ -84,7 +99,7 @@
 
 def step_kernel(
     frames, conv_1, proj_1, conv_2, proj_2, out_grad,
-    out_frames, frame_grad, totals,
+    out_frames, frame_grad, conv_total_2, proj_total_2, conv_total_1, proj_total_1,
     w1, w2, q1, q2, xs, mid, s2, t1, t2, g, gmid, gp1, gp2, slope_t, slope_g,
     tap_in, tap_out, near_tap, pre2, wide,
     xs_in, mid_in, s2_in, t1_in, t2_in, gp2_in, g_in, gp1_in, gm_in,
@@ -128,8 +143,7 @@
     for j in range(4):
         for copy in conv_loads(j):
             copy.start()
-    for name in ("q1", "w2", "g", "q2"):
-        loads[name].start()
+    loads["q1"].start()
 
     barrier = pltpu.get_barrier_semaphore()
     for peer in peers + (other_core, far_y, next_peer, prev_peer):
@@ -234,6 +248,9 @@
                 for copy in conv_loads(j):
                     copy.wait()
                 gate_tile(j)
+                if j == 0:
+                    for name in ("w2", "g", "q2"):
+                        loads[name].start()
             loads["q1"].wait()
         else:
             tiles(4, gate_tile)
@@ -307,7 +324,16 @@
 
     tiles(4, current_tile)
 
-    sums, arrivals = (acc2, w2), (got2, got1)
+    def units(start, count):
+        return pl.ds(pl.multiple_of(start * UNIT, UNIT), count * UNIT)
+
+    def ours(b, slab, rows):
+        if b == 0:
+            return acc2.at[slab, rows, :]
+        return w2.at[rows, slab * TILE : slab * TILE + TILE]
+
+    def theirs(b, slab, rows):
+        return (got2, got1)[b].at[slab, rows, :]
 
     def weight_products(b):
         if b == 0:
@@ -318,8 +344,6 @@
             lefts = ((xs, 0, xs_in), (xs, NEAR, xs_in), (t1, 0, t1_in))
             own_p, own_g = half(gp1, core, 1024), half(gmid, core, 512)
             pre_in, grad_in = gp1_in, gm_in
-        bounds = color_bounds(b)
-
         def product_tile(m):
             for part, (own, low, theirs) in enumerate(lefts):
                 span = slice(low, low + ROWS)
@@ -349,74 +373,60 @@
                             (row // 2) % 2,
                             row % 2,
                         )
-                        for color, (begin, end) in enumerate(bounds):
-                            begin, end = max(begin, first), min(end, first + 512)
-                            if begin >= end:
-                                continue
+                        for local in range(2):
+                            slab = first // TILE + local
                             spot = 0
-                            for step, dim in enumerate(order_of(color)):
+                            for step, dim in enumerate(ORDERS[b][slab]):
                                 spot = spot + unit[dim] * 2 ** (5 - step)
-                            place_rows = pl.ds(pl.multiple_of(spot * UNIT, UNIT), UNIT)
-                            sums[b][place_rows, begin:end] = product[
-                                row * 16 : row * 16 + 16, begin - first : end - first
+                            ours(b, slab, units(spot, 1))[...] = product[
+                                row * 16 : row * 16 + 16, local * TILE : local * TILE + TILE
                             ]
 
         tiles(4, product_tile)
 
-    def ranges(color, step):
+    def ranges(b, slab, step):
         base = 0
-        for earlier, dim in enumerate(order_of(color)[:step]):
+        for earlier, dim in enumerate(ORDERS[b][slab][:step]):
             base = base + bits[dim] * 2 ** (5 - earlier)
         count = 2 ** (5 - step)
-        mine = bits[order_of(color)[step]]
+        mine = bits[ORDERS[b][slab][step]]
         return base + mine * count, base + (1 - mine) * count, count
 
-    def units(start, count):
-        return pl.ds(pl.multiple_of(start * UNIT, UNIT), count * UNIT)
-
-    def reduce_copy(b, color, step, landing):
-        begin, end = color_bounds(b)[color]
-        keep, give, count = ranges(color, step)
-        target = keep if landing else give
+    def reduce_copy(b, slab, step, landing):
+        keep, give, count = ranges(b, slab, step)
         return remote(
-            sums[b].at[units(give, count), begin:end],
-            arrivals[b].at[units(target, count), begin:end],
-            rs_send.at[b, color, step], rs_recv.at[b, color, step],
-            peers[order_of(color)[step]],
+            ours(b, slab, units(give, count)),
+            theirs(b, slab, units(keep if landing else give, count)),
+            rs_send.at[b, slab, step], rs_recv.at[b, slab, step],
+            peers[ORDERS[b][slab][step]],
         )
 
     yh, xh, xq = bits[2], bits[4], bits[5]
 
-    def fold(b, color, step):
-        begin, end = color_bounds(b)[color]
-        keep, give, count = ranges(color, step)
-        chunk = min(count, 4)
-        ours, theirs = sums[b], arrivals[b]
+    def fold(b, slab, step):
+        keep, give, count = ranges(b, slab, step)
+        chunk = min(count, 16)
 
         def total(i):
-            here = ours[units(keep + i * chunk, chunk), begin:end]
-            there = theirs[units(give + i * chunk, chunk), begin:end]
-            return (here.astype(f32) + there.astype(f32)).astype(bf16)
+            here = ours(b, slab, units(keep + i * chunk, chunk))[...]
+            return here + theirs(b, slab, units(give + i * chunk, chunk))[...]
 
         if step == 5:
-            full[b, core, yh, xh, xq, :, begin:end] = total(0)
+            full[b, core, yh, xh, xq, :, slab * TILE : slab * TILE + TILE] = total(0)
             return
-
-        def put(i):
-            ours[units(keep + i * chunk, chunk), begin:end] = total(i)
-
-        tiles(count // chunk, put)
+        for i in range(count // chunk):
+            ours(b, slab, units(keep + i * chunk, chunk))[...] = total(i)
 
     def advance(b, step):
-        for color in range(6):
-            reduce_copy(b, color, step, False).wait_recv()
-            fold(b, color, step)
+        for slab in range(SLABS):
+            reduce_copy(b, slab, step, False).wait_recv()
+            fold(b, slab, step)
             if step < 5:
-                reduce_copy(b, color, step + 1, True).start()
+                reduce_copy(b, slab, step + 1, True).start()
 
     def begin_reduce(b):
-        for color in range(6):
-            reduce_copy(b, color, 0, True).start()
+        for slab in range(SLABS):
+            reduce_copy(b, slab, 0, True).start()
 
     for name in ("mid", "s2", "t2", "gp2", "g"):
         for copy in swaps[name]:
@@ -444,13 +454,12 @@
 
     for c in range(CHUNKS):
         first_backward(c)
-    advance(0, 0)
     for name in ("x", "halo", "t1", "gp1", "gm"):
         for copy in swaps[name]:
             copy.wait_recv()
     weight_products(1)
     begin_reduce(1)
-    advance(0, 1)
+    advance(0, 0)
 
     for copy in far_back:
         copy.wait_send()
@@ -461,14 +470,13 @@
 
     tiles(4, first_tap_tile)
     near_back.start()
-    advance(0, 2)
+    advance(0, 1)
 
     def first_current_tile(j):
         value = dot_nt(gp1[...], w1[columns(j * TILE), 2 * WIDTH : 4 * WIDTH])
         pre2[:, columns(j * TILE)] = value + gmid[:, columns(j * TILE)].astype(f32)
 
     tiles(4, first_current_tile)
-    advance(0, 3)
     for copy in far_forward + swaps["mid"]:
         copy.wait_send()
 
@@ -480,7 +488,7 @@
     store_out = pltpu.make_async_copy(mid, out_frames.at[0], st_sem.at[0])
     store_out.start()
     advance(1, 0)
-    advance(0, 4)
+    advance(0, 2)
     near_back.wait_recv()
     for copy in swaps["gm"]:
         copy.wait_send()
@@ -499,43 +507,67 @@
         ref = full.at[(b, core) + where]
         return remote(ref, ref, ag_send.at[b, index], ag_recv.at[b, index], target)
 
+    places = (
+        ((yh, xh, xq), far_y),
+        ((every, xh, xq, every, left), peers[5]),
+        ((every, xh, xq, every, right), peers[4]),
+        ((every, xh, every, every, left), peers[4]),
+        ((every, every, xq, every, right), peers[5]),
+        ((every, xh, xq), other_core),
+        ((every, xh, 1 - xq, every, left), other_core),
+        ((every, 1 - xh, xq, every, right), other_core),
+        ((every, 1 - xh, every, every, left), other_core),
+        ((every, every, 1 - xq, every, right), other_core),
+    )
+
     def gather(b, index):
-        if index == 0:
-            return gather_copy(b, 0, (yh, xh, xq), far_y)
-        if index == 1:
-            return gather_copy(b, 1, (every, xh, xq, every, left), peers[5])
-        if index == 2:
-            return gather_copy(b, 2, (every, xh, xq, every, right), peers[4])
-        if index == 3:
-            return gather_copy(b, 3, (every, xh, every, every, left), peers[4])
-        if index == 4:
-            return gather_copy(b, 4, (every, every, xq, every, right), peers[5])
-        return gather_copy(b, 5, (), other_core)
+        return gather_copy(b, index, *places[index])
+
+    def stores(b):
+        conv, proj = ((conv_total_2, proj_total_2), (conv_total_1, proj_total_1))[b]
+        copies = []
+        for k in range(2):
+            moves = (
+                (conv, k * 1024, 0, 1024),
+                (conv, 2048 + k * 1024, 1024, 1024),
+                (proj, k * 512, 2048, 512),
+            )
+            for target, to, start, width in moves:
+                copies.append(
+                    pltpu.make_async_copy(
+                        full.at[b, k, :, :, :, :, start : start + width],
+                        target.at[:, :, :, :, to : to + width],
+                        st_sem.at[2 + b * 6 + len(copies)],
+                    )
+                )
+        return copies
 
     def gather_stage(b, stage):
-        waits = ((), (0,), (1, 2), (3, 4), (5,))[stage]
-        starts = ((0,), (1, 2), (3, 4), (5,), ())[stage]
+        waits = ((), (0,), (1, 2), (3, 4), (5, 6, 7, 8, 9))[stage]
+        starts = ((0,), (1, 2, 5), (3, 4, 6, 7), (8, 9), ())[stage]
         for index in waits:
             gather(b, index).wait_recv()
         for index in starts:
             gather(b, index).start()
         if stage == 4:
-            pltpu.make_async_copy(full.at[b], totals.at[b], st_sem.at[2 + b]).start()
+            for copy in stores(b):
+                copy.start()
 
     advance(1, 1)
+    advance(0, 3)
+    advance(1, 2)
+    advance(0, 4)
+    advance(1, 3)
     advance(0, 5)
     gather_stage(0, 0)
-    advance(1, 2)
+    advance(1, 4)
     gather_stage(0, 1)
-    advance(1, 3)
-    gather_stage(0, 2)
-    advance(1, 4)
-    gather_stage(0, 3)
     advance(1, 5)
     gather_stage(1, 0)
-    gather_stage(0, 4)
-    for stage in range(1, 5):
-        gather_stage(1, stage)
+    for stage in range(2, 5):
+        gather_stage(0, stage)
+        gather_stage(1, stage - 1)
+    gather_stage(1, 4)
 
     near_forward.wait_send()
     near_back.wait_send()
@@ -544,12 +576,13 @@
             for copy in copies:
                 copy.wait_send()
     for b in range(2):
-        for index in range(6):
+        for index in range(10):
             gather(b, index).wait_send()
-        for color in range(6):
+        for slab in range(SLABS):
             for step in range(6):
-                reduce_copy(b, color, step, True).wait_send()
-        pltpu.make_async_copy(full.at[b], totals.at[b], st_sem.at[2 + b]).wait()
+                reduce_copy(b, slab, step, True).wait_send()
+        for copy in stores(b):
+            copy.wait()
     store_out.wait()
     store_grad.wait()
 
@@ -559,19 +592,21 @@
     bf16, f32 = jnp.bfloat16, jnp.float32
     frame_shape = jax.ShapeDtypeStruct((1, ROWS, WIDTH), bf16)
     totals_shape = (2, 2, 2, 2, 2, UNIT, HALF)
+    conv_shape = jax.ShapeDtypeStruct((2, 2, 2, UNIT, 4 * WIDTH), bf16)
+    proj_shape = jax.ShapeDtypeStruct((2, 2, 2, UNIT, WIDTH), bf16)
     frame = pltpu.VMEM((ROWS, WIDTH), bf16)
     double = pltpu.VMEM((ROWS, 2 * WIDTH), bf16)
     narrow = pltpu.VMEM((ROWS, WIDTH // 2), bf16)
     weight = pltpu.VMEM((WIDTH, 4 * WIDTH), bf16)
     square = pltpu.VMEM((WIDTH, WIDTH), bf16)
     padded = pltpu.VMEM((ROWS + NEAR, WIDTH), bf16)
-    share = pltpu.VMEM((WIDTH, HALF), bf16)
+    share = pltpu.VMEM((SLABS, WIDTH, TILE), bf16)
     dma = pltpu.SemaphoreType.DMA
     return pl.pallas_call(
         step_kernel,
-        out_shape=[frame_shape, frame_shape, jax.ShapeDtypeStruct(totals_shape, bf16)],
+        out_shape=[frame_shape, frame_shape] + [conv_shape, proj_shape] * 2,
         in_specs=[anywhere] * 6,
-        out_specs=[anywhere] * 3,
+        out_specs=[anywhere] * 6,
         scratch_shapes=[
             weight, weight, square, square,
             padded, frame, frame, frame, frame, frame, frame,
@@ -582,7 +617,7 @@
             share, share, share, pltpu.VMEM(totals_shape, bf16),
             dma((21,)), dma((2,)), dma((2,)), dma((2, CHUNKS)), dma((2, CHUNKS)),
             dma((10, CHUNKS)), dma((10, CHUNKS)),
-            dma((2, 6, 6)), dma((2, 6, 6)), dma((2, 6)), dma((2, 6)), dma((4,)),
+            dma((2, SLABS, 6)), dma((2, SLABS, 6)), dma((2, 10)), dma((2, 10)), dma((14,)),
         ],
         compiler_params=pltpu.CompilerParams(
             collective_id=0, has_side_effects=True, vmem_limit_bytes=67043328
@@ -590,30 +625,16 @@
     )(*operands)
 
 
-def scaled(total, rows):
-    scale = float(
-        lax.axis_size("dp") * lax.axis_size(("tx", "ty")) * rows
-    ) ** (-0.5)
-    total = total.reshape(2, 128, HALF)
-    value = total.astype(jnp.float32) * scale
-    conv = jnp.concatenate(
-        [value[0, :, :1024], value[1, :, :1024], value[0, :, 1024:2048], value[1, :, 1024:2048]], 1
-    )
-    return conv, jnp.concatenate([value[0, :, 2048:], value[1, :, 2048:]], 1)
+def scaled(total):
+    count = lax.axis_size("dp") * lax.axis_size(("tx", "ty")) * ROWS
+    value = total.astype(jnp.float32) * float(count) ** (-0.5)
+    return value.reshape(128, total.shape[-1])
 
 
 def shards(*operands):
-    block_output, input_gradient, totals = whole_step(*operands)
-    conv_two_grad, proj_two_grad = scaled(totals[0], ROWS)
-    conv_one_grad, proj_one_grad = scaled(totals[1], ROWS)
-    return (
-        block_output,
-        input_gradient,
-        conv_one_grad,
-        proj_one_grad,
-        conv_two_grad,
-        proj_two_grad,
-    )
+    block_output, input_gradient, *totals = whole_step(*operands)
+    conv_two, proj_two, conv_one, proj_one = (scaled(total) for total in totals)
+    return (block_output, input_gradient, conv_one, proj_one, conv_two, proj_two)
 
 
 def solution(mesh):

time: 141 us -> 139 us (0.986)
    concatenate x2 -> x0, other arithmetic: 3.52 us -> none  [the longest x1 2.46 us: scaled(): jnp.concatenate([value[0, :, :1024], value[1, :, :1024], value[0, :, 1024...]
    mul x1 -> x2, other arithmetic: 2.43 us -> 5.2 us  [scaled(): value = total.astype(jnp.float32) * float(count) ** (-0.5)]
where the time goes in v3:
time: 139 us
  Pallas kernels  131 us (94%)
  other arithmetic  5.2 us (4%)
  local copies, waits for them, and re-layouts  1.99 us (1%)
    pallas_call x1, Pallas kernels, whole_step(): pl.pallas_call(step_kernel, out_shape=[frame_shape, frame_shape] + [conv_...  131 us
    mul x2, other arithmetic, scaled(): value = total.astype(jnp.float32) * float(count) ** (-0.5)  5.2 us

profile of v3, /device:TPU:1, one launch (start us, length us, event | category | flops | bytes accessed | tf_op | source)
XLA Modules:
  0.0 138.6 jit_solution(4451408825739399454)
XLA Ops:
  0.6 130.7 %shard_map.109 = (bf16[1,384,1024]{2,1,0:T(8,128)(2,1)}, bf16[1,384,1024]{2,1,0:T(8,128)(2,1)}, bf16[2,2,2,16,4096]{4,3,2,1,0:T(8,128)(2,1)}, bf16[2,2,2,16,1024...) custom-call(bf16[1,384,1024]{2,1,0:T(8,128)(2,1)} %frames.1, ...), custom_call_target="tpu_custom_call" | custom-call | tf_op jit(solution)/shard_map/pallas_call | solution.py:605
  131.4 0.0 copy-start.2
  131.4 0.0 copy-start.3
  131.4 4.1 %convert_multiply_fusion = (f32[2,2,2,16,4096]{4,3,2,1,0:T(8,128)}, f32[2,2,2,16,4096]{4,3,2,1,0:T(8,128)}) fusion(bf16[2,2,2,16,4096]{4,3,2,1,0:T(8,128)(2,1)} %get-tuple-element.16, bf16[2,2,2,16,4096]{4,3,2,1,0:T(8,128)(2,1)} %get-tuple-element.14), kind=kLoop, calls=%fused_computation | loop fusion | flops 2097152 | bytes 6291456 | tf_op jit(solution)/shard_map/mul | solution.py:630
  135.5 0.0 copy-start.1
  135.5 0.0 copy-start
  135.5 0.0 copy-done.2
  135.5 0.0 copy-done.3
  135.5 1.1 convert_multiply_fusion.2
  136.6 0.2 copy-done.1
  136.8 0.9 copy.14
  137.7 0.0 copy-done
  137.7 0.9 copy.15
Async XLA Ops:
  131.4 4.1 %copy-start.2 = (bf16[2,2,2,16,1024]{4,3,2,1,0:T(8,128)(2,1)S(1)}, bf16[2,2,2,16,1024]{4,3,2,1,0:T(8,128)(2,1)}, u32[]{:S(2)}) copy-start(bf16[2,2,2,16,1024]{4,3,2,1,0:T(8,128)(2,1)} %get-tuple-element.17) | copy-start | bytes 786436
  131.4 4.1 %copy-start.3 = (bf16[2,2,2,16,1024]{4,3,2,1,0:T(8,128)(2,1)S(1)}, bf16[2,2,2,16,1024]{4,3,2,1,0:T(8,128)(2,1)}, u32[]{:S(2)}) copy-start(bf16[2,2,2,16,1024]{4,3,2,1,0:T(8,128)(2,1)} %get-tuple-element.15) | copy-start | bytes 786436
  135.5 1.3 copy-start.1
  135.5 2.2 %copy-start = (bf16[1,384,1024]{2,1,0:T(8,128)(2,1)S(1)}, bf16[1,384,1024]{2,1,0:T(8,128)(2,1)}, u32[]{:S(2)}) copy-start(bf16[1,384,1024]{2,1,0:T(8,128)(2,1)} %get-tuple-element.29) | copy-start | bytes 2359300

commit v4 on v3

--- a/solution.py
+++ b/solution.py
@@ -8,9 +8,11 @@
 NEAR = 64
 ROWS = 384
 WIDTH = 1024
-CHUNKS = 2
+CHUNKS = 4
 CHUNK = ROWS // CHUNKS
 TILE = 256
+HALVES = 2
+HALF_ROWS = ROWS // HALVES
 
 MESH = pl.DeviceIdType.MESH
 UNIT = 16
@@ -164,6 +166,7 @@
     every = slice(None)
     top = pl.ds(0, NEAR)
     parts = [pl.ds(c * CHUNK, CHUNK) for c in range(CHUNKS)]
+    halves = [pl.ds(c * HALF_ROWS, HALF_ROWS) for c in range(HALVES)]
     swaps = {
         "x": [swap(0, 0, frames.at[0], xs_in.at[pl.ds(NEAR, ROWS), :])],
         "halo": [swap(1, 0, xs.at[top, :], xs_in.at[top, :])],
@@ -176,12 +179,17 @@
             swap(item, c, source.at[rows, :], target.at[rows, :])
             for c, rows in enumerate(parts)
         ]
-    for item, (name, source, target, width) in enumerate(
-        (("gp2", gp2, gp2_in, 1024), ("gp1", gp1, gp1_in, 1024), ("gm", gmid, gm_in, 512)), 7
+    for item, (name, source, target, width, pieces) in enumerate(
+        (
+            ("gp2", gp2, gp2_in, 1024, parts),
+            ("gp1", gp1, gp1_in, 1024, halves),
+            ("gm", gmid, gm_in, 512, halves),
+        ),
+        7,
     ):
         swaps[name] = [
             swap(item, c, half_rows(source, 1 - core, width, rows), target.at[rows, :])
-            for c, rows in enumerate(parts)
+            for c, rows in enumerate(pieces)
         ]
 
     near_forward = remote(
@@ -318,12 +326,6 @@
     for c in range(CHUNKS):
         second_block(c)
 
-    def current_tile(j):
-        value = dot_nt(gp2[...], w2[columns(j * TILE), 2 * WIDTH : 4 * WIDTH])
-        wide[:, columns(j * TILE)] = value + g[:, columns(j * TILE)].astype(f32)
-
-    tiles(4, current_tile)
-
     def units(start, count):
         return pl.ds(pl.multiple_of(start * UNIT, UNIT), count * UNIT)
 
@@ -335,7 +337,7 @@
     def theirs(b, slab, rows):
         return (got2, got1)[b].at[slab, rows, :]
 
-    def weight_products(b):
+    def weight_products(b, part):
         if b == 0:
             lefts = ((s2, 0, s2_in), (mid, 0, mid_in), (t2, 0, t2_in))
             own_p, own_g = half(gp2, core, 1024), half(g, core, 512)
@@ -345,42 +347,42 @@
             own_p, own_g = half(gp1, core, 1024), half(gmid, core, 512)
             pre_in, grad_in = gp1_in, gm_in
         def product_tile(m):
-            for part, (own, low, theirs) in enumerate(lefts):
-                span = slice(low, low + ROWS)
-                left = jnp.concatenate(
-                    [own[span, columns(m * TILE)], theirs[span, columns(m * TILE)]], 0
-                )
-                for piece in range(2 if part < 2 else 1):
-                    lo = piece * 512
-                    if part < 2:
-                        right = jnp.concatenate(
-                            [own_p[:, lo : lo + 512], pre_in[:, lo : lo + 512]], 0
-                        )
-                    else:
-                        right = jnp.concatenate([own_g[...], grad_in[...]], 0)
-                    product = dot_tn(left, right).astype(bf16)
-                    first = part * 1024 + lo
-                    for row in range(16):
-                        block = 2 * m + row // 8
-                        y_lo, z = lax.div(block, 4), lax.rem(block, 4)
-                        zh = lax.div(z, 2)
-                        side = (row // 4) % 2
-                        unit = (
-                            zh,
-                            lax.rem(zh + z, 2),
-                            side,
-                            lax.rem(side + y_lo, 2),
-                            (row // 2) % 2,
-                            row % 2,
-                        )
-                        for local in range(2):
-                            slab = first // TILE + local
-                            spot = 0
-                            for step, dim in enumerate(ORDERS[b][slab]):
-                                spot = spot + unit[dim] * 2 ** (5 - step)
-                            ours(b, slab, units(spot, 1))[...] = product[
-                                row * 16 : row * 16 + 16, local * TILE : local * TILE + TILE
-                            ]
+            own, low, partner = lefts[part]
+            span = slice(low, low + ROWS)
+            left = jnp.concatenate(
+                [own[span, columns(m * TILE)], partner[span, columns(m * TILE)]], 0
+            )
+            for piece in range(2 if part < 2 else 1):
+                lo = piece * 512
+                if part < 2:
+                    right = jnp.concatenate(
+                        [own_p[:, lo : lo + 512], pre_in[:, lo : lo + 512]], 0
+                    )
+                else:
+                    right = jnp.concatenate([own_g[...], grad_in[...]], 0)
+                product = dot_tn(left, right).astype(bf16)
+                first = part * 1024 + lo
+                for row in range(16):
+                    block = 2 * m + row // 8
+                    y_lo, z = lax.div(block, 4), lax.rem(block, 4)
+                    zh = lax.div(z, 2)
+                    side = (row // 4) % 2
+                    unit = (
+                        zh,
+                        lax.rem(zh + z, 2),
+                        side,
+                        lax.rem(side + y_lo, 2),
+                        (row // 2) % 2,
+                        row % 2,
+                    )
+                    for local in range(2):
+                        slab = first // TILE + local
+                        spot = 0
+                        for step, dim in enumerate(ORDERS[b][slab]):
+                            spot = spot + unit[dim] * 2 ** (5 - step)
+                        ours(b, slab, units(spot, 1))[...] = product[
+                            row * 16 : row * 16 + 16, local * TILE : local * TILE + TILE
+                        ]
 
         tiles(4, product_tile)
 
@@ -417,27 +419,38 @@
         for i in range(count // chunk):
             ours(b, slab, units(keep + i * chunk, chunk))[...] = total(i)
 
-    def advance(b, step):
-        for slab in range(SLABS):
+    def slabs_of(part):
+        return range(4 * part, min(4 * part + 4, SLABS))
+
+    def advance(b, step, slabs=range(SLABS)):
+        for slab in slabs:
             reduce_copy(b, slab, step, False).wait_recv()
             fold(b, slab, step)
             if step < 5:
                 reduce_copy(b, slab, step + 1, True).start()
 
-    def begin_reduce(b):
-        for slab in range(SLABS):
+    def begin_reduce(b, part):
+        for slab in slabs_of(part):
             reduce_copy(b, slab, 0, True).start()
 
     for name in ("mid", "s2", "t2", "gp2", "g"):
         for copy in swaps[name]:
             copy.wait_recv()
-    weight_products(0)
-    begin_reduce(0)
+    for part in range(3):
+        weight_products(0, part)
+        begin_reduce(0, part)
+
+    def current_tile(j):
+        value = dot_nt(gp2[...], w2[columns(j * TILE), 2 * WIDTH : 4 * WIDTH])
+        wide[:, columns(j * TILE)] = value + g[:, columns(j * TILE)].astype(f32)
+
+    tiles(4, current_tile)
 
     def first_backward(c):
-        low = c * CHUNK
-        rows = slice(low, low + CHUNK)
-        far_back[c].wait_recv()
+        low = c * HALF_ROWS
+        rows = slice(low, low + HALF_ROWS)
+        for copy in far_back[c * CHUNKS // HALVES : (c + 1) * CHUNKS // HALVES]:
+            copy.wait_recv()
         tap = tap_in[rows, :].astype(f32)
         total = wide[rows, :] + jnp.where(tx == 3, 0.0, tap)
         gmid[rows, :] = total.astype(bf16)
@@ -452,14 +465,25 @@
         tiles(4, slope_tile)
         swaps["gp1"][c].start()
 
-    for c in range(CHUNKS):
+    for c in range(HALVES):
         first_backward(c)
+    for copy in far_forward + swaps["mid"]:
+        copy.wait_send()
+
+    def second_out_tile(j):
+        value = dot_nn(t2[...], q2[:, columns(j * TILE)])
+        mid[:, columns(j * TILE)] = (value + mid[:, columns(j * TILE)].astype(f32)).astype(bf16)
+
+    tiles(4, second_out_tile)
+    store_out = pltpu.make_async_copy(mid, out_frames.at[0], st_sem.at[0])
+    store_out.start()
     for name in ("x", "halo", "t1", "gp1", "gm"):
         for copy in swaps[name]:
             copy.wait_recv()
-    weight_products(1)
-    begin_reduce(1)
-    advance(0, 0)
+    for part in range(3):
+        weight_products(1, part)
+        begin_reduce(1, part)
+        advance(0, 0, slabs_of(part))
 
     for copy in far_back:
         copy.wait_send()
@@ -470,23 +494,13 @@
 
     tiles(4, first_tap_tile)
     near_back.start()
-    advance(0, 1)
 
     def first_current_tile(j):
         value = dot_nt(gp1[...], w1[columns(j * TILE), 2 * WIDTH : 4 * WIDTH])
         pre2[:, columns(j * TILE)] = value + gmid[:, columns(j * TILE)].astype(f32)
 
     tiles(4, first_current_tile)
-    for copy in far_forward + swaps["mid"]:
-        copy.wait_send()
-
-    def second_out_tile(j):
-        value = dot_nn(t2[...], q2[:, columns(j * TILE)])
-        mid[:, columns(j * TILE)] = (value + mid[:, columns(j * TILE)].astype(f32)).astype(bf16)
-
-    tiles(4, second_out_tile)
-    store_out = pltpu.make_async_copy(mid, out_frames.at[0], st_sem.at[0])
-    store_out.start()
+    advance(0, 1)
     advance(1, 0)
     advance(0, 2)
     near_back.wait_recv()

time: 139 us -> 139 us (level)
  no operation moved by 1% of the time
where the time goes in v4:
time: 139 us
  Pallas kernels  131 us (94%)
  other arithmetic  5.2 us (4%)
  local copies, waits for them, and re-layouts  1.99 us (1%)
    pallas_call x1, Pallas kernels, whole_step(): pl.pallas_call(step_kernel, out_shape=[frame_shape, frame_shape] + [conv_...  131 us
    mul x2, other arithmetic, scaled(): value = total.astype(jnp.float32) * float(count) ** (-0.5)  5.2 us

profile of v4, /device:TPU:1, one launch (start us, length us, event | category | flops | bytes accessed | tf_op | source)
XLA Modules:
  0.0 139.2 jit_solution(13677530491171151928)
XLA Ops:
  0.6 131.4 %shard_map.109 = (bf16[1,384,1024]{2,1,0:T(8,128)(2,1)}, bf16[1,384,1024]{2,1,0:T(8,128)(2,1)}, bf16[2,2,2,16,4096]{4,3,2,1,0:T(8,128)(2,1)}, bf16[2,2,2,16,1024...) custom-call(bf16[1,384,1024]{2,1,0:T(8,128)(2,1)} %frames.1, ...), custom_call_target="tpu_custom_call" | custom-call | tf_op jit(solution)/shard_map/pallas_call | solution.py:619
  132.0 0.0 copy-start.2
  132.0 0.0 copy-start.3
  132.0 4.1 %convert_multiply_fusion = (f32[2,2,2,16,4096]{4,3,2,1,0:T(8,128)}, f32[2,2,2,16,4096]{4,3,2,1,0:T(8,128)}) fusion(bf16[2,2,2,16,4096]{4,3,2,1,0:T(8,128)(2,1)} %get-tuple-element.16, bf16[2,2,2,16,4096]{4,3,2,1,0:T(8,128)(2,1)} %get-tuple-element.14), kind=kLoop, calls=%fused_computation | loop fusion | flops 2097152 | bytes 6291456 | tf_op jit(solution)/shard_map/mul | solution.py:644
  136.1 0.0 copy-start.1
  136.1 0.0 copy-start
  136.1 0.0 copy-done.2
  136.1 0.0 copy-done.3
  136.2 1.1 convert_multiply_fusion.2
  137.2 0.2 copy-done.1
  137.5 0.9 copy.14
  138.3 0.0 copy-done
  138.3 0.9 copy.15
Async XLA Ops:
  132.0 4.1 %copy-start.2 = (bf16[2,2,2,16,1024]{4,3,2,1,0:T(8,128)(2,1)S(1)}, bf16[2,2,2,16,1024]{4,3,2,1,0:T(8,128)(2,1)}, u32[]{:S(2)}) copy-start(bf16[2,2,2,16,1024]{4,3,2,1,0:T(8,128)(2,1)} %get-tuple-element.17) | copy-start | bytes 786436
  132.0 4.1 %copy-start.3 = (bf16[2,2,2,16,1024]{4,3,2,1,0:T(8,128)(2,1)S(1)}, bf16[2,2,2,16,1024]{4,3,2,1,0:T(8,128)(2,1)}, u32[]{:S(2)}) copy-start(bf16[2,2,2,16,1024]{4,3,2,1,0:T(8,128)(2,1)} %get-tuple-element.15) | copy-start | bytes 786436
  136.1 1.3 copy-start.1
  136.1 2.2 %copy-start = (bf16[1,384,1024]{2,1,0:T(8,128)(2,1)S(1)}, bf16[1,384,1024]{2,1,0:T(8,128)(2,1)}, u32[]{:S(2)}) copy-start(bf16[1,384,1024]{2,1,0:T(8,128)(2,1)} %get-tuple-element.29) | copy-start | bytes 2359300

commit v5 on v4

--- a/solution.py
+++ b/solution.py
@@ -8,9 +8,10 @@
 NEAR = 64
 ROWS = 384
 WIDTH = 1024
-CHUNKS = 4
+CHUNKS = 3
 CHUNK = ROWS // CHUNKS
 TILE = 256
+BROAD = 512
 HALVES = 2
 HALF_ROWS = ROWS // HALVES
 
@@ -126,6 +127,9 @@
     def columns(start):
         return pl.ds(pl.multiple_of(start, TILE), TILE)
 
+    def broad(start):
+        return pl.ds(pl.multiple_of(start, BROAD), BROAD)
+
     def conv_loads(j):
         return [
             load(
@@ -141,16 +145,20 @@
     loads["w2"] = load(18, conv_2, w2)
     loads["g"] = load(19, out_grad.at[0], g)
     loads["q2"] = load(20, proj_2, q2)
+    barrier = pltpu.get_barrier_semaphore()
+    for peer in peers + (other_core, far_y, next_peer, prev_peer):
+        pl.semaphore_signal(barrier, inc=1, device_id=peer, device_id_type=MESH)
     loads["x"].start()
+    pl.semaphore_wait(barrier, 10)
+    near_forward = remote(
+        frames.at[0, pl.ds(ROWS - NEAR, NEAR), :], xs.at[pl.ds(0, NEAR), :],
+        near_send.at[0], near_recv.at[0], next_peer,
+    )
+    near_forward.start()
     for j in range(4):
         for copy in conv_loads(j):
             copy.start()
     loads["q1"].start()
-
-    barrier = pltpu.get_barrier_semaphore()
-    for peer in peers + (other_core, far_y, next_peer, prev_peer):
-        pl.semaphore_signal(barrier, inc=1, device_id=peer, device_id_type=MESH)
-    pl.semaphore_wait(barrier, 10)
 
     def half(ref, which, width):
         return ref.at[:, pl.ds(pl.multiple_of(which * width, width), width)]
@@ -192,10 +200,6 @@
             for c, rows in enumerate(pieces)
         ]
 
-    near_forward = remote(
-        frames.at[0, pl.ds(ROWS - NEAR, NEAR), :], xs.at[top, :],
-        near_send.at[0], near_recv.at[0], next_peer,
-    )
     near_back = remote(
         tap_out.at[top, :], near_tap, near_send.at[1], near_recv.at[1], prev_peer
     )
@@ -213,17 +217,20 @@
         for c, rows in enumerate(parts)
     ]
 
-    near_forward.start()
-    swaps["x"][0].start()
-    swaps["g"][0].start()
     loads["x"].wait()
-    near_forward.wait_recv()
-
-    @pl.when(first_shard)
-    def _():
-        xs[0:NEAR, :] = jnp.zeros((NEAR, WIDTH), bf16)
-
-    swaps["halo"][0].start()
+
+    def share_inputs():
+        swaps["x"][0].start()
+        swaps["g"][0].start()
+
+    def take_halo():
+        near_forward.wait_recv()
+
+        @pl.when(first_shard)
+        def _():
+            xs[0:NEAR, :] = jnp.zeros((NEAR, WIDTH), bf16)
+
+        swaps["halo"][0].start()
 
     def tiles(count, body):
         def step(j, carry):
@@ -251,7 +258,7 @@
             slope_t[rows, columns(start)] = (gt * (1.0 - th * th)).astype(bf16)
             slope_g[rows, columns(start)] = (th * gt * (1.0 - gt)).astype(bf16)
 
-        if c == 0:
+        if c == 1:
             for j in range(4):
                 for copy in conv_loads(j):
                     copy.wait()
@@ -260,7 +267,10 @@
                     for name in ("w2", "g", "q2"):
                         loads[name].start()
             loads["q1"].wait()
+            share_inputs()
         else:
+            if c == 0:
+                take_halo()
             tiles(4, gate_tile)
         swaps["t1"][c].start()
 
@@ -273,22 +283,23 @@
         far_forward[c].start()
         swaps["mid"][c].start()
 
-    for c in range(CHUNKS):
+    turns = (1, 2, 0)
+    for c in turns:
         first_forward(c)
 
     loads["w2"].wait()
 
     def pre_tile(j):
-        pre2[:, columns(j * TILE)] = dot_nn(mid[...], w2[:, columns(2 * WIDTH + j * TILE)])
-
-    tiles(8, pre_tile)
+        pre2[:, broad(j * BROAD)] = dot_nn(mid[...], w2[:, broad(2 * WIDTH + j * BROAD)])
+
+    tiles(4, pre_tile)
     loads["g"].wait()
     loads["q2"].wait()
 
     def gated_grad_tile(j):
-        wide[:, columns(j * TILE)] = dot_nt(g[...], q2[columns(j * TILE), :])
-
-    tiles(4, gated_grad_tile)
+        wide[:, broad(j * BROAD)] = dot_nt(g[...], q2[broad(j * BROAD), :])
+
+    tiles(2, gated_grad_tile)
 
     def second_block(c):
         low = c * CHUNK
@@ -323,7 +334,7 @@
         tiles(4, tap_tile)
         far_back[c].start()
 
-    for c in range(CHUNKS):
+    for c in turns:
         second_block(c)
 
     def units(start, count):
@@ -399,7 +410,7 @@
         return remote(
             ours(b, slab, units(give, count)),
             theirs(b, slab, units(keep if landing else give, count)),
-            rs_send.at[b, slab, step], rs_recv.at[b, slab, step],
+            rs_send.at[b, slab, step % 2], rs_recv.at[b, slab, step],
             peers[ORDERS[b][slab][step]],
         )
 
@@ -428,6 +439,8 @@
             fold(b, slab, step)
             if step < 5:
                 reduce_copy(b, slab, step + 1, True).start()
+        for slab in slabs:
+            reduce_copy(b, slab, step, True).wait_send()
 
     def begin_reduce(b, part):
         for slab in slabs_of(part):
@@ -441,16 +454,14 @@
         begin_reduce(0, part)
 
     def current_tile(j):
-        value = dot_nt(gp2[...], w2[columns(j * TILE), 2 * WIDTH : 4 * WIDTH])
-        wide[:, columns(j * TILE)] = value + g[:, columns(j * TILE)].astype(f32)
-
-    tiles(4, current_tile)
+        value = dot_nt(gp2[...], w2[broad(j * BROAD), 2 * WIDTH : 4 * WIDTH])
+        wide[:, broad(j * BROAD)] = value + g[:, broad(j * BROAD)].astype(f32)
+
+    tiles(2, current_tile)
 
     def first_backward(c):
         low = c * HALF_ROWS
         rows = slice(low, low + HALF_ROWS)
-        for copy in far_back[c * CHUNKS // HALVES : (c + 1) * CHUNKS // HALVES]:
-            copy.wait_recv()
         tap = tap_in[rows, :].astype(f32)
         total = wide[rows, :] + jnp.where(tx == 3, 0.0, tap)
         gmid[rows, :] = total.astype(bf16)
@@ -465,42 +476,44 @@
         tiles(4, slope_tile)
         swaps["gp1"][c].start()
 
+    for copy in far_back:
+        copy.wait_recv()
     for c in range(HALVES):
         first_backward(c)
     for copy in far_forward + swaps["mid"]:
         copy.wait_send()
 
     def second_out_tile(j):
-        value = dot_nn(t2[...], q2[:, columns(j * TILE)])
-        mid[:, columns(j * TILE)] = (value + mid[:, columns(j * TILE)].astype(f32)).astype(bf16)
-
-    tiles(4, second_out_tile)
+        value = dot_nn(t2[...], q2[:, broad(j * BROAD)])
+        mid[:, broad(j * BROAD)] = (value + mid[:, broad(j * BROAD)].astype(f32)).astype(bf16)
+
+    tiles(2, second_out_tile)
     store_out = pltpu.make_async_copy(mid, out_frames.at[0], st_sem.at[0])
     store_out.start()
+    advance(0, 0)
     for name in ("x", "halo", "t1", "gp1", "gm"):
         for copy in swaps[name]:
             copy.wait_recv()
     for part in range(3):
         weight_products(1, part)
         begin_reduce(1, part)
-        advance(0, 0, slabs_of(part))
+    advance(0, 1)
 
     for copy in far_back:
         copy.wait_send()
 
     def first_tap_tile(j):
-        value = dot_nt(gp1[...], w1[columns(j * TILE), 0 : 2 * WIDTH])
-        tap_out[:, columns(j * TILE)] = value.astype(bf16)
-
-    tiles(4, first_tap_tile)
+        value = dot_nt(gp1[...], w1[broad(j * BROAD), 0 : 2 * WIDTH])
+        tap_out[:, broad(j * BROAD)] = value.astype(bf16)
+
+    tiles(2, first_tap_tile)
     near_back.start()
 
     def first_current_tile(j):
-        value = dot_nt(gp1[...], w1[columns(j * TILE), 2 * WIDTH : 4 * WIDTH])
-        pre2[:, columns(j * TILE)] = value + gmid[:, columns(j * TILE)].astype(f32)
-
-    tiles(4, first_current_tile)
-    advance(0, 1)
+        value = dot_nt(gp1[...], w1[broad(j * BROAD), 2 * WIDTH : 4 * WIDTH])
+        pre2[:, broad(j * BROAD)] = value + gmid[:, broad(j * BROAD)].astype(f32)
+
+    tiles(2, first_current_tile)
     advance(1, 0)
     advance(0, 2)
     near_back.wait_recv()
@@ -567,38 +580,35 @@
             for copy in stores(b):
                 copy.start()
 
-    advance(1, 1)
-    advance(0, 3)
-    advance(1, 2)
-    advance(0, 4)
-    advance(1, 3)
-    advance(0, 5)
+    for step in range(1, 4):
+        advance(1, step)
+        advance(0, step + 2)
     gather_stage(0, 0)
     advance(1, 4)
-    gather_stage(0, 1)
     advance(1, 5)
     gather_stage(1, 0)
-    for stage in range(2, 5):
-        gather_stage(0, stage)
-        gather_stage(1, stage - 1)
-    gather_stage(1, 4)
-
+    gather_stage(0, 1)
+    gather_stage(1, 1)
+    gather_stage(0, 2)
+    gather_stage(1, 2)
+    gather_stage(0, 3)
     near_forward.wait_send()
     near_back.wait_send()
     for name, copies in swaps.items():
         if name not in ("mid", "gm"):
             for copy in copies:
                 copy.wait_send()
+    store_out.wait()
+    store_grad.wait()
+    gather_stage(0, 4)
+    gather_stage(1, 3)
+    gather_stage(1, 4)
+
     for b in range(2):
         for index in range(10):
             gather(b, index).wait_send()
-        for slab in range(SLABS):
-            for step in range(6):
-                reduce_copy(b, slab, step, True).wait_send()
         for copy in stores(b):
             copy.wait()
-    store_out.wait()
-    store_grad.wait()
 
 
 def whole_step(*operands):
@@ -631,7 +641,7 @@
             share, share, share, pltpu.VMEM(totals_shape, bf16),
             dma((21,)), dma((2,)), dma((2,)), dma((2, CHUNKS)), dma((2, CHUNKS)),
             dma((10, CHUNKS)), dma((10, CHUNKS)),
-            dma((2, SLABS, 6)), dma((2, SLABS, 6)), dma((2, 10)), dma((2, 10)), dma((14,)),
+            dma((2, SLABS, 2)), dma((2, SLABS, 6)), dma((2, 10)), dma((2, 10)), dma((14,)),
         ],
         compiler_params=pltpu.CompilerParams(
             collective_id=0, has_side_effects=True, vmem_limit_bytes=67043328

time: 139 us -> 125 us (0.90)
  Pallas kernels: 131 us -> 117 us
    pallas_call x1, Pallas kernels: 131 us -> 117 us  [whole_step(): pl.pallas_call(step_kernel, out_shape=[frame_shape, frame_shape] + [conv_...]
where the time goes in v5:
time: 125 us
  Pallas kernels  117 us (94%)
  other arithmetic  5.2 us (4%)
  local copies, waits for them, and re-layouts  1.99 us (2%)
    pallas_call x1, Pallas kernels, whole_step(): pl.pallas_call(step_kernel, out_shape=[frame_shape, frame_shape] + [conv_...  117 us
    mul x2, other arithmetic, scaled(): value = total.astype(jnp.float32) * float(count) ** (-0.5)  5.2 us

profile of v5, /device:TPU:1, one launch (start us, length us, event | category | flops | bytes accessed | tf_op | source)
XLA Modules:
  0.0 124.8 jit_solution(11197532578493398154)
XLA Ops:
  0.6 117.0 %shard_map.109 = (bf16[1,384,1024]{2,1,0:T(8,128)(2,1)}, bf16[1,384,1024]{2,1,0:T(8,128)(2,1)}, bf16[2,2,2,16,4096]{4,3,2,1,0:T(8,128)(2,1)}, bf16[2,2,2,16,1024...) custom-call(bf16[1,384,1024]{2,1,0:T(8,128)(2,1)} %frames.1, ...), custom_call_target="tpu_custom_call" | custom-call | tf_op jit(solution)/shard_map/pallas_call | solution.py:629
  117.6 0.0 copy-start.2
  117.6 0.0 copy-start.3
  117.6 4.1 %convert_multiply_fusion = (f32[2,2,2,16,4096]{4,3,2,1,0:T(8,128)}, f32[2,2,2,16,4096]{4,3,2,1,0:T(8,128)}) fusion(bf16[2,2,2,16,4096]{4,3,2,1,0:T(8,128)(2,1)} %get-tuple-element.16, bf16[2,2,2,16,4096]{4,3,2,1,0:T(8,128)(2,1)} %get-tuple-element.14), kind=kLoop, calls=%fused_computation | loop fusion | flops 2097152 | bytes 6291456 | tf_op jit(solution)/shard_map/mul | solution.py:654
  121.7 0.0 copy-start.1
  121.7 0.0 copy-start
  121.7 0.0 copy-done.2
  121.8 0.0 copy-done.3
  121.8 1.1 convert_multiply_fusion.2
  122.9 0.2 copy-done.1
  123.1 0.9 copy.14
  123.9 0.0 copy-done
  123.9 0.9 copy.15
Async XLA Ops:
  117.6 4.1 %copy-start.2 = (bf16[2,2,2,16,1024]{4,3,2,1,0:T(8,128)(2,1)S(1)}, bf16[2,2,2,16,1024]{4,3,2,1,0:T(8,128)(2,1)}, u32[]{:S(2)}) copy-start(bf16[2,2,2,16,1024]{4,3,2,1,0:T(8,128)(2,1)} %get-tuple-element.17) | copy-start | bytes 786436
  117.6 4.1 %copy-start.3 = (bf16[2,2,2,16,1024]{4,3,2,1,0:T(8,128)(2,1)S(1)}, bf16[2,2,2,16,1024]{4,3,2,1,0:T(8,128)(2,1)}, u32[]{:S(2)}) copy-start(bf16[2,2,2,16,1024]{4,3,2,1,0:T(8,128)(2,1)} %get-tuple-element.15) | copy-start | bytes 786436
  121.7 1.3 %copy-start.1 = (bf16[1,384,1024]{2,1,0:T(8,128)(2,1)S(1)}, bf16[1,384,1024]{2,1,0:T(8,128)(2,1)}, u32[]{:S(2)}) copy-start(bf16[1,384,1024]{2,1,0:T(8,128)(2,1)} %get-tuple-element.28) | copy-start | bytes 2359300
  121.7 2.2 %copy-start = (bf16[1,384,1024]{2,1,0:T(8,128)(2,1)S(1)}, bf16[1,384,1024]{2,1,0:T(8,128)(2,1)}, u32[]{:S(2)}) copy-start(bf16[1,384,1024]{2,1,0:T(8,128)(2,1)} %get-tuple-element.29) | copy-start | bytes 2359300

commit v6 on v5

--- a/solution.py
+++ b/solution.py
@@ -18,31 +18,52 @@
 MESH = pl.DeviceIdType.MESH
 UNIT = 16
 HALF = 2560
-SLABS = 10
+SLABS = 20
+SLAB = 128
 ORDERS = (
     (
-        (0, 2, 1, 4, 3, 5),
-        (1, 5, 2, 3, 0, 4),
-        (2, 0, 3, 5, 4, 1),
-        (3, 1, 0, 2, 4, 5),
-        (4, 5, 3, 1, 2, 0),
-        (5, 3, 0, 2, 1, 4),
-        (0, 3, 4, 5, 1, 2),
-        (1, 5, 4, 2, 3, 0),
-        (2, 4, 1, 5, 0, 3),
-        (4, 3, 5, 0, 2, 1),
+        (0, 3, 5, 2, 4, 1),
+        (1, 5, 2, 0, 3, 4),
+        (2, 5, 4, 1, 0, 3),
+        (3, 4, 0, 2, 1, 5),
+        (4, 3, 1, 5, 0, 2),
+        (5, 3, 1, 0, 4, 2),
+        (0, 4, 5, 3, 2, 1),
+        (1, 0, 2, 4, 5, 3),
+        (2, 0, 3, 1, 4, 5),
+        (3, 4, 5, 2, 1, 0),
+        (4, 2, 3, 0, 5, 1),
+        (5, 4, 2, 0, 1, 3),
+        (0, 1, 3, 4, 2, 5),
+        (1, 2, 5, 3, 4, 0),
+        (2, 5, 0, 1, 3, 4),
+        (3, 5, 1, 4, 2, 0),
+        (4, 3, 0, 2, 5, 1),
+        (5, 2, 4, 1, 0, 3),
+        (0, 1, 3, 4, 2, 5),
+        (1, 2, 4, 5, 3, 0),
     ),
     (
-        (1, 3, 5, 2, 4, 0),
-        (0, 5, 3, 4, 2, 1),
-        (3, 0, 1, 4, 5, 2),
-        (2, 4, 0, 3, 1, 5),
-        (5, 2, 1, 3, 0, 4),
-        (4, 2, 5, 1, 0, 3),
-        (1, 4, 3, 2, 0, 5),
-        (0, 1, 2, 4, 5, 3),
-        (3, 2, 0, 4, 1, 5),
-        (5, 4, 2, 0, 1, 3),
+        (2, 4, 3, 1, 0, 5),
+        (3, 4, 2, 1, 5, 0),
+        (4, 5, 1, 0, 2, 3),
+        (5, 0, 2, 4, 1, 3),
+        (0, 1, 5, 4, 3, 2),
+        (1, 2, 4, 3, 0, 5),
+        (2, 1, 4, 3, 5, 0),
+        (3, 0, 2, 4, 1, 5),
+        (4, 2, 5, 1, 3, 0),
+        (5, 0, 3, 1, 4, 2),
+        (0, 3, 1, 5, 4, 2),
+        (1, 3, 0, 5, 2, 4),
+        (2, 0, 5, 3, 4, 1),
+        (3, 5, 4, 2, 0, 1),
+        (4, 1, 0, 2, 5, 3),
+        (5, 1, 0, 4, 3, 2),
+        (0, 5, 1, 3, 2, 4),
+        (1, 5, 3, 2, 4, 0),
+        (2, 4, 5, 0, 1, 3),
+        (3, 4, 0, 2, 1, 5),
     ),
 )
 
@@ -134,8 +155,8 @@
         return [
             load(
                 4 * j + part,
-                conv_1.at[:, pl.ds(part * WIDTH + j * TILE, TILE)],
-                w1.at[:, pl.ds(part * WIDTH + j * TILE, TILE)],
+                conv_1.at[:, pl.ds(part * WIDTH + j * BROAD, BROAD)],
+                w1.at[:, pl.ds(part * WIDTH + j * BROAD, BROAD)],
             )
             for part in range(4)
         ]
@@ -155,7 +176,7 @@
         near_send.at[0], near_recv.at[0], next_peer,
     )
     near_forward.start()
-    for j in range(4):
+    for j in range(2):
         for copy in conv_loads(j):
             copy.start()
     loads["q1"].start()
@@ -246,20 +267,20 @@
 
         def gate_tile(j):
             old, now = xs[rows, :], xs[moved, :]
-            start = j * TILE
-            a = dot_nn(old, w1[:, columns(start)]) + dot_nn(
-                now, w1[:, columns(2 * WIDTH + start)]
+            start = j * BROAD
+            a = dot_nn(old, w1[:, broad(start)]) + dot_nn(
+                now, w1[:, broad(2 * WIDTH + start)]
             )
-            v = dot_nn(old, w1[:, columns(WIDTH + start)]) + dot_nn(
-                now, w1[:, columns(3 * WIDTH + start)]
+            v = dot_nn(old, w1[:, broad(WIDTH + start)]) + dot_nn(
+                now, w1[:, broad(3 * WIDTH + start)]
             )
             th, gt = jnp.tanh(a), jax.nn.sigmoid(v)
-            t1[rows, columns(start)] = (th * gt).astype(bf16)
-            slope_t[rows, columns(start)] = (gt * (1.0 - th * th)).astype(bf16)
-            slope_g[rows, columns(start)] = (th * gt * (1.0 - gt)).astype(bf16)
+            t1[rows, broad(start)] = (th * gt).astype(bf16)
+            slope_t[rows, broad(start)] = (gt * (1.0 - th * th)).astype(bf16)
+            slope_g[rows, broad(start)] = (th * gt * (1.0 - gt)).astype(bf16)
 
         if c == 1:
-            for j in range(4):
+            for j in range(2):
                 for copy in conv_loads(j):
                     copy.wait()
                 gate_tile(j)
@@ -271,15 +292,15 @@
         else:
             if c == 0:
                 take_halo()
-            tiles(4, gate_tile)
+            tiles(2, gate_tile)
         swaps["t1"][c].start()
 
         def out_tile(j):
-            value = dot_nn(t1[rows, :], q1[:, columns(j * TILE)])
-            value = value + xs[moved, columns(j * TILE)].astype(f32)
-            mid[rows, columns(j * TILE)] = value.astype(bf16)
-
-        tiles(4, out_tile)
+            value = dot_nn(t1[rows, :], q1[:, broad(j * BROAD)])
+            value = value + xs[moved, broad(j * BROAD)].astype(f32)
+            mid[rows, broad(j * BROAD)] = value.astype(bf16)
+
+        tiles(2, out_tile)
         far_forward[c].start()
         swaps["mid"][c].start()
 
@@ -314,7 +335,7 @@
 
         def gate_tile(j):
             old = s2[rows, :]
-            here, there = columns(j * TILE), columns(WIDTH + j * TILE)
+            here, there = broad(j * BROAD), broad(WIDTH + j * BROAD)
             a = dot_nn(old, w2[:, here]) + pre2[rows, here]
             v = dot_nn(old, w2[:, there]) + pre2[rows, there]
             th, gt = jnp.tanh(a), jax.nn.sigmoid(v)
@@ -323,15 +344,15 @@
             gp2[rows, here] = (grad * (1.0 - th * th)).astype(bf16)
             gp2[rows, there] = (grad * th * (1.0 - gt)).astype(bf16)
 
-        tiles(4, gate_tile)
+        tiles(2, gate_tile)
         swaps["t2"][c].start()
         swaps["gp2"][c].start()
 
         def tap_tile(j):
-            value = dot_nt(gp2[rows, :], w2[columns(j * TILE), 0 : 2 * WIDTH])
-            tap_out[rows, columns(j * TILE)] = value.astype(bf16)
-
-        tiles(4, tap_tile)
+            value = dot_nt(gp2[rows, :], w2[broad(j * BROAD), 0 : 2 * WIDTH])
+            tap_out[rows, broad(j * BROAD)] = value.astype(bf16)
+
+        tiles(2, tap_tile)
         far_back[c].start()
 
     for c in turns:
@@ -341,12 +362,10 @@
         return pl.ds(pl.multiple_of(start * UNIT, UNIT), count * UNIT)
 
     def ours(b, slab, rows):
-        if b == 0:
-            return acc2.at[slab, rows, :]
-        return w2.at[rows, slab * TILE : slab * TILE + TILE]
+        return (acc2, w2)[b].at[rows, slab * SLAB : slab * SLAB + SLAB]
 
     def theirs(b, slab, rows):
-        return (got2, got1)[b].at[slab, rows, :]
+        return (got2, got1)[b].at[rows, slab * SLAB : slab * SLAB + SLAB]
 
     def weight_products(b, part):
         if b == 0:
@@ -378,21 +397,17 @@
                     y_lo, z = lax.div(block, 4), lax.rem(block, 4)
                     zh = lax.div(z, 2)
                     side = (row // 4) % 2
-                    unit = (
-                        zh,
-                        lax.rem(zh + z, 2),
-                        side,
-                        lax.rem(side + y_lo, 2),
-                        (row // 2) % 2,
-                        row % 2,
-                    )
-                    for local in range(2):
-                        slab = first // TILE + local
-                        spot = 0
-                        for step, dim in enumerate(ORDERS[b][slab]):
-                            spot = spot + unit[dim] * 2 ** (5 - step)
+                    moving = {0: zh, 1: lax.rem(zh + z, 2), 3: lax.rem(side + y_lo, 2)}
+                    fixed = {2: side, 4: (row // 2) % 2, 5: row % 2}
+                    for local in range(512 // SLAB):
+                        slab = first // SLAB + local
+                        weight = {
+                            dim: 2 ** (5 - step) for step, dim in enumerate(ORDERS[b][slab])
+                        }
+                        spot = sum(moving[dim] * weight[dim] for dim in moving)
+                        spot = spot + sum(fixed[dim] * weight[dim] for dim in fixed)
                         ours(b, slab, units(spot, 1))[...] = product[
-                            row * 16 : row * 16 + 16, local * TILE : local * TILE + TILE
+                            row * 16 : row * 16 + 16, local * SLAB : local * SLAB + SLAB
                         ]
 
         tiles(4, product_tile)
@@ -418,20 +433,20 @@
 
     def fold(b, slab, step):
         keep, give, count = ranges(b, slab, step)
-        chunk = min(count, 16)
+        chunk = min(count, 32)
 
         def total(i):
             here = ours(b, slab, units(keep + i * chunk, chunk))[...]
             return here + theirs(b, slab, units(give + i * chunk, chunk))[...]
 
         if step == 5:
-            full[b, core, yh, xh, xq, :, slab * TILE : slab * TILE + TILE] = total(0)
+            full[b, core, yh, xh, xq, :, slab * SLAB : slab * SLAB + SLAB] = total(0)
             return
         for i in range(count // chunk):
             ours(b, slab, units(keep + i * chunk, chunk))[...] = total(i)
 
     def slabs_of(part):
-        return range(4 * part, min(4 * part + 4, SLABS))
+        return range(8 * part, min(8 * part + 8, SLABS))
 
     def advance(b, step, slabs=range(SLABS)):
         for slab in slabs:
@@ -468,12 +483,12 @@
         swaps["gm"][c].start()
 
         def slope_tile(j):
-            here, there = columns(j * TILE), columns(WIDTH + j * TILE)
+            here, there = broad(j * BROAD), broad(WIDTH + j * BROAD)
             grad = dot_nt(gmid[rows, :], q1[here, :])
             gp1[rows, here] = (grad * slope_t[rows, here].astype(f32)).astype(bf16)
             gp1[rows, there] = (grad * slope_g[rows, here].astype(f32)).astype(bf16)
 
-        tiles(4, slope_tile)
+        tiles(2, slope_tile)
         swaps["gp1"][c].start()
 
     for copy in far_back:
@@ -490,14 +505,13 @@
     tiles(2, second_out_tile)
     store_out = pltpu.make_async_copy(mid, out_frames.at[0], st_sem.at[0])
     store_out.start()
-    advance(0, 0)
     for name in ("x", "halo", "t1", "gp1", "gm"):
         for copy in swaps[name]:
             copy.wait_recv()
     for part in range(3):
         weight_products(1, part)
         begin_reduce(1, part)
-    advance(0, 1)
+    advance(0, 0)
 
     for copy in far_back:
         copy.wait_send()
@@ -515,7 +529,7 @@
 
     tiles(2, first_current_tile)
     advance(1, 0)
-    advance(0, 2)
+    advance(0, 1)
     near_back.wait_recv()
     for copy in swaps["gm"]:
         copy.wait_send()
@@ -553,7 +567,7 @@
     def stores(b):
         conv, proj = ((conv_total_2, proj_total_2), (conv_total_1, proj_total_1))[b]
         copies = []
-        for k in range(2):
+        for k in (core, 1 - core):
             moves = (
                 (conv, k * 1024, 0, 1024),
                 (conv, 2048 + k * 1024, 1024, 1024),
@@ -563,7 +577,7 @@
                 copies.append(
                     pltpu.make_async_copy(
                         full.at[b, k, :, :, :, :, start : start + width],
-                        target.at[:, :, :, :, to : to + width],
+                        target.at[:, :, :, :, pl.ds(pl.multiple_of(to, width), width)],
                         st_sem.at[2 + b * 6 + len(copies)],
                     )
                 )
@@ -576,15 +590,14 @@
             gather(b, index).wait_recv()
         for index in starts:
             gather(b, index).start()
-        if stage == 4:
-            for copy in stores(b):
+        if stage >= 3:
+            for copy in stores(b)[3 * stage - 9 : 3 * stage - 6]:
                 copy.start()
 
-    for step in range(1, 4):
+    for step in range(1, 5):
         advance(1, step)
-        advance(0, step + 2)
+        advance(0, step + 1)
     gather_stage(0, 0)
-    advance(1, 4)
     advance(1, 5)
     gather_stage(1, 0)
     gather_stage(0, 1)
@@ -624,7 +637,7 @@
     weight = pltpu.VMEM((WIDTH, 4 * WIDTH), bf16)
     square = pltpu.VMEM((WIDTH, WIDTH), bf16)
     padded = pltpu.VMEM((ROWS + NEAR, WIDTH), bf16)
-    share = pltpu.VMEM((SLABS, WIDTH, TILE), bf16)
+    share = pltpu.VMEM((WIDTH, HALF), bf16)
     dma = pltpu.SemaphoreType.DMA
     return pl.pallas_call(
         step_kernel,

time: 125 us -> 120 us (0.960)
  Pallas kernels: 117 us -> 112 us
    pallas_call x1, Pallas kernels: 117 us -> 112 us  [whole_step(): pl.pallas_call(step_kernel, out_shape=[frame_shape, frame_shape] + [conv_...]
where the time goes in v6:
time: 120 us
  Pallas kernels  112 us (93%)
  other arithmetic  5.2 us (4%)
  local copies, waits for them, and re-layouts  1.99 us (2%)
    pallas_call x1, Pallas kernels, whole_step(): pl.pallas_call(step_kernel, out_shape=[frame_shape, frame_shape] + [conv_...  112 us
    mul x2, other arithmetic, scaled(): value = total.astype(jnp.float32) * float(count) ** (-0.5)  5.2 us

profile of v6, /device:TPU:1, one launch (start us, length us, event | category | flops | bytes accessed | tf_op | source)
XLA Modules:
  0.0 119.6 jit_solution(16694425707871924132)
XLA Ops:
  0.6 111.8 %shard_map.109 = (bf16[1,384,1024]{2,1,0:T(8,128)(2,1)}, bf16[1,384,1024]{2,1,0:T(8,128)(2,1)}, bf16[2,2,2,16,4096]{4,3,2,1,0:T(8,128)(2,1)}, bf16[2,2,2,16,1024...) custom-call(bf16[1,384,1024]{2,1,0:T(8,128)(2,1)} %frames.1, ...), custom_call_target="tpu_custom_call" | custom-call | tf_op jit(solution)/shard_map/pallas_call | solution.py:642
  112.4 0.0 copy-start.2
  112.4 0.0 copy-start.3
  112.4 4.1 %convert_multiply_fusion = (f32[2,2,2,16,4096]{4,3,2,1,0:T(8,128)}, f32[2,2,2,16,4096]{4,3,2,1,0:T(8,128)}) fusion(bf16[2,2,2,16,4096]{4,3,2,1,0:T(8,128)(2,1)} %get-tuple-element.16, bf16[2,2,2,16,4096]{4,3,2,1,0:T(8,128)(2,1)} %get-tuple-element.14), kind=kLoop, calls=%fused_computation | loop fusion | flops 2097152 | bytes 6291456 | tf_op jit(solution)/shard_map/mul | solution.py:667
  116.5 0.0 copy-start.1
  116.5 0.0 copy-start
  116.5 0.0 copy-done.2
  116.5 0.0 copy-done.3
  116.6 1.1 convert_multiply_fusion.2
  117.6 0.2 copy-done.1
  117.9 0.9 copy.14
  118.7 0.0 copy-done
  118.7 0.9 copy.15
Async XLA Ops:
  112.4 4.1 %copy-start.2 = (bf16[2,2,2,16,1024]{4,3,2,1,0:T(8,128)(2,1)S(1)}, bf16[2,2,2,16,1024]{4,3,2,1,0:T(8,128)(2,1)}, u32[]{:S(2)}) copy-start(bf16[2,2,2,16,1024]{4,3,2,1,0:T(8,128)(2,1)} %get-tuple-element.17) | copy-start | bytes 786436
  112.4 4.1 %copy-start.3 = (bf16[2,2,2,16,1024]{4,3,2,1,0:T(8,128)(2,1)S(1)}, bf16[2,2,2,16,1024]{4,3,2,1,0:T(8,128)(2,1)}, u32[]{:S(2)}) copy-start(bf16[2,2,2,16,1024]{4,3,2,1,0:T(8,128)(2,1)} %get-tuple-element.15) | copy-start | bytes 786436
  116.5 1.3 %copy-start.1 = (bf16[1,384,1024]{2,1,0:T(8,128)(2,1)S(1)}, bf16[1,384,1024]{2,1,0:T(8,128)(2,1)}, u32[]{:S(2)}) copy-start(bf16[1,384,1024]{2,1,0:T(8,128)(2,1)} %get-tuple-element.28) | copy-start | bytes 2359300
  116.5 2.2 %copy-start = (bf16[1,384,1024]{2,1,0:T(8,128)(2,1)S(1)}, bf16[1,384,1024]{2,1,0:T(8,128)(2,1)}, u32[]{:S(2)}) copy-start(bf16[1,384,1024]{2,1,0:T(8,128)(2,1)} %get-tuple-element.29) | copy-start | bytes 2359300

commit v7 on v6

--- a/solution.py
+++ b/solution.py
@@ -425,8 +425,16 @@
         return remote(
             ours(b, slab, units(give, count)),
             theirs(b, slab, units(keep if landing else give, count)),
-            rs_send.at[b, slab, step % 2], rs_recv.at[b, slab, step],
+            rs_send.at[b, step % 2],
+            rs_recv.at[b, step * SLABS + slab if step < 2 else 2 * SLABS + step - 2],
             peers[ORDERS[b][slab][step]],
+        )
+
+    def reduce_step(b, step):
+        rows = pl.ds(0, 2 ** (5 - step) * UNIT)
+        return remote(
+            (acc2, w2)[b].at[rows, 0:HALF], (got2, got1)[b].at[rows, :],
+            rs_send.at[b, step % 2], rs_recv.at[b, 2 * SLABS + max(step, 2) - 2], other_core,
         )
 
     yh, xh, xq = bits[2], bits[4], bits[5]
@@ -448,14 +456,16 @@
     def slabs_of(part):
         return range(8 * part, min(8 * part + 8, SLABS))
 
-    def advance(b, step, slabs=range(SLABS)):
-        for slab in slabs:
-            reduce_copy(b, slab, step, False).wait_recv()
+    def advance(b, step):
+        if step >= 2:
+            reduce_step(b, step).wait_recv()
+        for slab in range(SLABS):
+            if step < 2:
+                reduce_copy(b, slab, step, False).wait_recv()
             fold(b, slab, step)
             if step < 5:
                 reduce_copy(b, slab, step + 1, True).start()
-        for slab in slabs:
-            reduce_copy(b, slab, step, True).wait_send()
+        reduce_step(b, step).wait_send()
 
     def begin_reduce(b, part):
         for slab in slabs_of(part):
@@ -548,21 +558,28 @@
         ref = full.at[(b, core) + where]
         return remote(ref, ref, ag_send.at[b, index], ag_recv.at[b, index], target)
 
-    places = (
-        ((yh, xh, xq), far_y),
-        ((every, xh, xq, every, left), peers[5]),
-        ((every, xh, xq, every, right), peers[4]),
-        ((every, xh, every, every, left), peers[4]),
-        ((every, every, xq, every, right), peers[5]),
-        ((every, xh, xq), other_core),
-        ((every, xh, 1 - xq, every, left), other_core),
-        ((every, 1 - xh, xq, every, right), other_core),
-        ((every, 1 - xh, every, every, left), other_core),
-        ((every, every, 1 - xq, every, right), other_core),
+    own = (yh, xh, xq)
+    beside, below = (yh, xh, 1 - xq), (yh, 1 - xh, xq)
+    across, far = (yh, 1 - xh, 1 - xq), (1 - yh, xh, xq)
+    far_beside, far_below = (1 - yh, xh, 1 - xq), (1 - yh, 1 - xh, xq)
+    far_across = (1 - yh, 1 - xh, 1 - xq)
+    moves_out = (
+        (own, far_y),
+        (own, peers[5]),
+        (own, peers[4]),
+        (far, peers[5]),
+        (far, peers[4]),
+        (beside + (every, left), peers[4]),
+        (below + (every, right), peers[5]),
+        (far_beside + (every, left), peers[4]),
+        (far_below + (every, right), peers[5]),
     )
 
     def gather(b, index):
-        return gather_copy(b, index, *places[index])
+        return gather_copy(b, index, *moves_out[index])
+
+    def share(b, where):
+        return gather_copy(b, 9, where, other_core)
 
     def stores(b):
         conv, proj = ((conv_total_2, proj_total_2), (conv_total_1, proj_total_1))[b]
@@ -584,14 +601,25 @@
         return copies
 
     def gather_stage(b, stage):
-        waits = ((), (0,), (1, 2), (3, 4), (5, 6, 7, 8, 9))[stage]
-        starts = ((0,), (1, 2, 5), (3, 4, 6, 7), (8, 9), ())[stage]
-        for index in waits:
-            gather(b, index).wait_recv()
-        for index in starts:
-            gather(b, index).start()
-        if stage >= 3:
-            for copy in stores(b)[3 * stage - 9 : 3 * stage - 6]:
+        plan = (
+            (((), (0, 1, 2), own),),
+            (((1,), (5,), beside), ((2,), (6,), below)),
+            (((0,), (3, 4), far),),
+            (((3,), (7,), far_beside), ((4,), (8,), far_below)),
+            (((5, 6), (), across),),
+            (((7, 8), (), far_across),),
+            (),
+        )[stage]
+        for waits, starts, piece in plan:
+            for index in waits:
+                gather(b, index).wait_recv()
+            for index in starts:
+                gather(b, index).start()
+            share(b, piece).start()
+        if stage == 6:
+            share(b, ()).wait_recv()
+        if stage >= 5:
+            for copy in stores(b)[3 * stage - 15 : 3 * stage - 12]:
                 copy.start()
 
     for step in range(1, 5):
@@ -600,11 +628,9 @@
     gather_stage(0, 0)
     advance(1, 5)
     gather_stage(1, 0)
-    gather_stage(0, 1)
-    gather_stage(1, 1)
-    gather_stage(0, 2)
-    gather_stage(1, 2)
-    gather_stage(0, 3)
+    for stage in range(1, 6):
+        gather_stage(0, stage)
+        gather_stage(1, stage)
     near_forward.wait_send()
     near_back.wait_send()
     for name, copies in swaps.items():
@@ -613,13 +639,13 @@
                 copy.wait_send()
     store_out.wait()
     store_grad.wait()
-    gather_stage(0, 4)
-    gather_stage(1, 3)
-    gather_stage(1, 4)
+    gather_stage(0, 6)
+    gather_stage(1, 6)
 
     for b in range(2):
-        for index in range(10):
+        for index in range(9):
             gather(b, index).wait_send()
+        share(b, ()).wait_send()
         for copy in stores(b):
             copy.wait()
 
@@ -654,7 +680,7 @@
             share, share, share, pltpu.VMEM(totals_shape, bf16),
             dma((21,)), dma((2,)), dma((2,)), dma((2, CHUNKS)), dma((2, CHUNKS)),
             dma((10, CHUNKS)), dma((10, CHUNKS)),
-            dma((2, SLABS, 2)), dma((2, SLABS, 6)), dma((2, 10)), dma((2, 10)), dma((14,)),
+            dma((2, 2)), dma((2, 2 * SLABS + 4)), dma((2, 10)), dma((2, 10)), dma((14,)),
         ],
         compiler_params=pltpu.CompilerParams(
             collective_id=0, has_side_effects=True, vmem_limit_bytes=67043328

time: 120 us -> 118 us (0.983)
  Pallas kernels: 112 us -> 110 us
    pallas_call x1, Pallas kernels: 112 us -> 110 us  [whole_step(): pl.pallas_call(step_kernel, out_shape=[frame_shape, frame_shape] + [conv_...]
where the time goes in v7:
time: 118 us
  Pallas kernels  110 us (93%)
  other arithmetic  5.2 us (4%)
  local copies, waits for them, and re-layouts  1.99 us (2%)
    pallas_call x1, Pallas kernels, whole_step(): pl.pallas_call(step_kernel, out_shape=[frame_shape, frame_shape] + [conv_...  110 us
    mul x2, other arithmetic, scaled(): value = total.astype(jnp.float32) * float(count) ** (-0.5)  5.2 us

profile of v7, /device:TPU:1, one launch (start us, length us, event | category | flops | bytes accessed | tf_op | source)
XLA Modules:
  0.0 117.7 jit_solution(9620517306695315641)
XLA Ops:
  0.6 109.8 %shard_map.109 = (bf16[1,384,1024]{2,1,0:T(8,128)(2,1)}, bf16[1,384,1024]{2,1,0:T(8,128)(2,1)}, bf16[2,2,2,16,4096]{4,3,2,1,0:T(8,128)(2,1)}, bf16[2,2,2,16,1024...) custom-call(bf16[1,384,1024]{2,1,0:T(8,128)(2,1)} %frames.1, ...), custom_call_target="tpu_custom_call" | custom-call | tf_op jit(solution)/shard_map/pallas_call | solution.py:668
  110.4 0.0 copy-start.2
  110.4 0.0 copy-start.3
  110.5 4.1 %convert_multiply_fusion = (f32[2,2,2,16,4096]{4,3,2,1,0:T(8,128)}, f32[2,2,2,16,4096]{4,3,2,1,0:T(8,128)}) fusion(bf16[2,2,2,16,4096]{4,3,2,1,0:T(8,128)(2,1)} %get-tuple-element.16, bf16[2,2,2,16,4096]{4,3,2,1,0:T(8,128)(2,1)} %get-tuple-element.14), kind=kLoop, calls=%fused_computation | loop fusion | flops 2097152 | bytes 6291456 | tf_op jit(solution)/shard_map/mul | solution.py:693
  114.6 0.0 copy-start.1
  114.6 0.0 copy-start
  114.6 0.0 copy-done.2
  114.6 0.0 copy-done.3
  114.6 1.1 convert_multiply_fusion.2
  115.7 0.2 copy-done.1
  115.9 0.9 copy.14
  116.8 0.0 copy-done
  116.8 0.9 copy.15
Async XLA Ops:
  110.4 4.1 %copy-start.2 = (bf16[2,2,2,16,1024]{4,3,2,1,0:T(8,128)(2,1)S(1)}, bf16[2,2,2,16,1024]{4,3,2,1,0:T(8,128)(2,1)}, u32[]{:S(2)}) copy-start(bf16[2,2,2,16,1024]{4,3,2,1,0:T(8,128)(2,1)} %get-tuple-element.17) | copy-start | bytes 786436
  110.4 4.1 %copy-start.3 = (bf16[2,2,2,16,1024]{4,3,2,1,0:T(8,128)(2,1)S(1)}, bf16[2,2,2,16,1024]{4,3,2,1,0:T(8,128)(2,1)}, u32[]{:S(2)}) copy-start(bf16[2,2,2,16,1024]{4,3,2,1,0:T(8,128)(2,1)} %get-tuple-element.15) | copy-start | bytes 786436
  114.6 1.3 %copy-start.1 = (bf16[1,384,1024]{2,1,0:T(8,128)(2,1)S(1)}, bf16[1,384,1024]{2,1,0:T(8,128)(2,1)}, u32[]{:S(2)}) copy-start(bf16[1,384,1024]{2,1,0:T(8,128)(2,1)} %get-tuple-element.28) | copy-start | bytes 2359300
  114.6 2.2 %copy-start = (bf16[1,384,1024]{2,1,0:T(8,128)(2,1)S(1)}, bf16[1,384,1024]{2,1,0:T(8,128)(2,1)}, u32[]{:S(2)}) copy-start(bf16[1,384,1024]{2,1,0:T(8,128)(2,1)} %get-tuple-element.29) | copy-start | bytes 2359300
